TPU v7x, 32 devices: a whole 2x2x4 slice. The times are simulated.
32 devices in a mesh: ctx: 16 (over z, y, core), shard: 2 (over x).
Axes of the slice: x: 2, y: 2, z: 4, core: 2. Of those that a mesh axis runs over, the one named last changes fastest.
Arguments:
- query: bfloat16 [4096, 2048], P('ctx', 'shard'), may hold values from -6 to 6
- key: bfloat16 [4096, 1024], P('ctx', 'shard'), may hold values from -6 to 6
- value: bfloat16 [4096, 1024], P('ctx', 'shard'), may hold values from -6 to 6
- attention_output: bfloat16 [4096, 2048], P('ctx', 'shard'), may hold values from -3 to 3
- grad_y: bfloat16 [4096, 2048], P('ctx'), may hold values from -24 to 24
- doc_ids: int32 [4096], P('ctx'), may hold values from 0 to 7, never falling along the last dimension, each value on 1 to 1024 neighbouring positions
- codes: bfloat16 [2048, 2048], P('shard', 'ctx'), may hold values from -0.125 to 0.125
- scale_copies: float32 [2, 16, 128], P('shard'), may hold values from 0.5 to 2
- holder: int32 [16], replicated, may hold values from 0 to 1
Outputs:
- grad_query: bfloat16 [4096, 2048], P('ctx', 'shard')
- key_gradient: bfloat16 [4096, 1024], P('ctx', 'shard')
- value_gradient: bfloat16 [4096, 1024], P('ctx', 'shard')
- grad_weight: float32 [2048, 2048], P('ctx', 'shard')
Inputs may be any that keep to these rules, and one draw needn't show every extreme that they name: doc_ids never falls along the sequence; each document holds 1 to 1024 positions, one exactly 1024. Only scale_copies[holder[p], p] is used for panel p.
All inputs are finite; a program needn't handle non-finite values.
Results may differ from a plain program's by a relative error of at most 0.008.
Values may be sent and summed in bfloat16 or wider, within the bound.
A program may use at most 64 MiB of HBM per device.

v0:
```python
import jax
import jax.numpy as jnp
from jax import lax
from jax.sharding import PartitionSpec as P

HEAD_WIDTH = 128


def from_behind(x, axis, by):
    size = lax.axis_size(axis)
    pairs = [(i, i + by) for i in range(size) if 0 <= i + by < size]
    return lax.ppermute(x, axis, pairs)


def shifted(block, axis, distance):
    devices = range(lax.axis_size(axis))
    route = [((i - distance) % len(devices), i) for i in devices]
    return lax.ppermute(block, axis, route)


def per_device(query, key, value, attention_output, grad_y, doc_ids, codes, scale_copies, holder):
    row_count = query.shape[0]
    heads_dev = query.shape[1] // HEAD_WIDTH
    groups = key.shape[1] // HEAD_WIDTH
    pairing_count = heads_dev // groups
    shard_index = lax.axis_index("shard")
    ctx_index = lax.axis_index("ctx")
    ctx_count = lax.axis_size("ctx")
    cycle_steps = ctx_count // 4 + 1
    score_scale = HEAD_WIDTH ** (-0.5)
    owned = (holder == shard_index)[:, None]
    scale_table = lax.psum(jnp.where(owned, scale_copies[0], 0.0), "shard")
    row_scale = lax.dynamic_slice_in_dim(
        scale_table, shard_index * heads_dev, heads_dev, 0
    ).reshape(heads_dev * HEAD_WIDTH)
    weight = (
        lax.all_gather(codes, "ctx", axis=1, tiled=True).astype(jnp.float32) * row_scale[:, None]
    ).astype(jnp.bfloat16)
    columns = grad_y
    attention_gradient = lax.dot_general(
        columns, weight, (((1,), (1,)), ((), ())), preferred_element_type=jnp.float32
    ).astype(jnp.bfloat16)
    columns = grad_y
    grad_weight = lax.psum_scatter(
        lax.dot_general(
            columns, attention_output, (((0,), (0,)), ((), ())), preferred_element_type=jnp.float32
        ),
        "ctx",
        scatter_dimension=0,
        tiled=True,
    ) * (row_count * ctx_count) ** (-0.5)
    head_queries = query.reshape(row_count, groups, pairing_count, HEAD_WIDTH)
    head_gradients = attention_gradient.reshape(row_count, groups, pairing_count, HEAD_WIDTH)
    output_heads = attention_output.reshape(row_count, groups, pairing_count, HEAD_WIDTH)
    head_keys = key.reshape(row_count, groups, HEAD_WIDTH)
    head_values = value.reshape(row_count, groups, HEAD_WIDTH)
    row_delta = jnp.sum(
        head_gradients.astype(jnp.float32) * output_heads.astype(jnp.float32), axis=-1
    ).transpose(1, 2, 0)
    offsets = jnp.arange(row_count, dtype=jnp.int32)

    def mask_for(query_index, key_index, query_docs, key_docs):
        query_pos = query_index * row_count + offsets
        key_pos = key_index * row_count + offsets
        return (key_pos[None, :] <= query_pos[:, None]) & (key_docs[None, :] == query_docs[:, None])

    def is_live(query_index, key_index, query_docs, key_docs):
        inside = (key_index >= 0) & (query_index < ctx_count)
        return inside & (key_index <= query_index) & (key_docs[row_count - 1] >= query_docs[0])

    def stats_update(softmax_stats, key_block, key_docs, key_index):

        def stats_live_branch(current):
            highest, running = current
            scores = (
                jnp.einsum(
                    "rgjd,ngd->gjrn", head_queries, key_block, preferred_element_type=jnp.float32
                )
                * score_scale
            )
            allowed = mask_for(ctx_index, key_index, doc_ids, key_docs)
            masked = jnp.where(allowed, scores, -1e30)
            newest = jnp.maximum(highest, jnp.max(masked, axis=-1))
            weights = jnp.where(allowed, jnp.exp(scores - newest[..., None]), 0.0)
            return (newest, running * jnp.exp(highest - newest) + jnp.sum(weights, axis=-1))

        return lax.cond(
            is_live(ctx_index, key_index, doc_ids, key_docs),
            stats_live_branch,
            lambda current: current,
            softmax_stats,
        )

    start_stats = (
        jnp.full((groups, pairing_count, row_count), -1e30, jnp.float32),
        jnp.zeros((groups, pairing_count, row_count), jnp.float32),
    )
    softmax_stats = stats_update(start_stats, head_keys, doc_ids, ctx_index)
    doc_table = jnp.zeros((cycle_steps, row_count), jnp.int32).at[0].set(doc_ids)

    def stats_step(cycle_step, loop_state):
        key_block, key_docs, softmax_stats, doc_table = loop_state
        key_block, key_docs = from_behind((key_block, key_docs), "ctx", 1)
        doc_table = lax.dynamic_update_index_in_dim(doc_table, key_docs, cycle_step, 0)
        softmax_stats = stats_update(softmax_stats, key_block, key_docs, ctx_index - cycle_step)
        return (key_block, key_docs, softmax_stats, doc_table)

    loop_state = lax.fori_loop(
        1, cycle_steps, stats_step, (head_keys, doc_ids, softmax_stats, doc_table)
    )
    softmax_stats = loop_state[2]
    doc_table = loop_state[3]
    log_total = softmax_stats[0] + jnp.log(softmax_stats[1])

    def tile_grads(query_block, grad_block, log_rows, delta_rows, key_block, value_block, allowed):
        scores = (
            jnp.einsum("rgjd,ngd->gjrn", query_block, key_block, preferred_element_type=jnp.float32)
            * score_scale
        )
        attention = jnp.where(allowed, jnp.exp(scores - log_rows[..., None]), 0.0)
        attention_low = attention.astype(jnp.bfloat16)
        attention_grad = jnp.einsum(
            "rgjd,ngd->gjrn", grad_block, value_block, preferred_element_type=jnp.float32
        )
        score_grad = (attention * (attention_grad - delta_rows[..., None])).astype(jnp.bfloat16)
        query_add = score_scale * jnp.einsum(
            "gjrn,ngd->rgjd", score_grad, key_block, preferred_element_type=jnp.float32
        )
        key_add = score_scale * jnp.einsum(
            "gjrn,rgjd->ngd", score_grad, query_block, preferred_element_type=jnp.float32
        )
        value_add = jnp.einsum(
            "gjrn,rgjd->ngd", attention_low, grad_block, preferred_element_type=jnp.float32
        )
        return (query_add, key_add, value_add)

    def add_tile(
        sums,
        query_index,
        key_index,
        query_docs,
        key_docs,
        query_block,
        grad_block,
        log_rows,
        delta_rows,
        key_block,
        value_block,
    ):

        def add_live_branch(current):
            allowed = mask_for(query_index, key_index, query_docs, key_docs)
            parts = tile_grads(
                query_block, grad_block, log_rows, delta_rows, key_block, value_block, allowed
            )
            return tuple((old + new for old, new in zip(current, parts)))

        return lax.cond(
            is_live(query_index, key_index, query_docs, key_docs),
            add_live_branch,
            lambda current: current,
            sums,
        )

    zeros_query = jnp.zeros((row_count, groups, pairing_count, HEAD_WIDTH), jnp.float32)
    zeros_key = jnp.zeros((row_count, groups, HEAD_WIDTH), jnp.float32)
    own_sums = add_tile(
        (zeros_query, zeros_key, zeros_key),
        ctx_index,
        ctx_index,
        doc_ids,
        doc_ids,
        head_queries,
        head_gradients,
        log_total,
        row_delta,
        head_keys,
        head_values,
    )

    def keys_step(cycle_step, loop_state):
        key_block, value_block, query_grad, key_grad, value_grad = loop_state
        key_block, value_block = from_behind((key_block, value_block), "ctx", 1)
        key_grad, value_grad = shifted((key_grad, value_grad), "ctx", 1)
        key_docs = lax.dynamic_index_in_dim(doc_table, cycle_step, 0, keepdims=False)
        query_grad, key_grad, value_grad = add_tile(
            (query_grad, key_grad, value_grad),
            ctx_index,
            ctx_index - cycle_step,
            doc_ids,
            key_docs,
            head_queries,
            head_gradients,
            log_total,
            row_delta,
            key_block,
            value_block,
        )
        return (key_block, value_block, query_grad, key_grad, value_grad)

    loop_state = lax.fori_loop(
        1, cycle_steps, keys_step, (head_keys, head_values, own_sums[0], own_sums[1], own_sums[2])
    )
    query_grad = loop_state[2]
    key_grad, value_grad = (
        shifted(loop_state[3].astype(jnp.bfloat16), "ctx", 1 - cycle_steps).astype(jnp.float32),
        shifted(loop_state[4].astype(jnp.bfloat16), "ctx", 1 - cycle_steps).astype(jnp.float32),
    )
    grad_query = query_grad.reshape(row_count, heads_dev * HEAD_WIDTH).astype(jnp.bfloat16)
    key_gradient = key_grad.reshape(row_count, groups * HEAD_WIDTH).astype(jnp.bfloat16)
    value_gradient = value_grad.reshape(row_count, groups * HEAD_WIDTH).astype(jnp.bfloat16)
    return (grad_query, key_gradient, value_gradient, grad_weight)


def solution(mesh):
    return jax.shard_map(
        per_device,
        mesh=mesh,
        in_specs=(
            P("ctx", "shard"),
            P("ctx", "shard"),
            P("ctx", "shard"),
            P("ctx", "shard"),
            P("ctx", None),
            P("ctx"),
            P("shard", "ctx"),
            P("shard", None, None),
            P(),
        ),
        out_specs=(P("ctx", "shard"), P("ctx", "shard"), P("ctx", "shard"), P("ctx", "shard")),
        check_vma=False,
    )
```

profile of v0, /device:TPU:0, one launch (start us, length us, event | category | flops | bytes accessed | tf_op | source)
XLA Modules:
  0.0 270.6 jit_solution(13765597213478499897)
XLA Ops:
  8.4 5.6 %fusion.45 = f32[2048,1024]{1,0:T(8,128)} fusion(bf16[256,2048]{1,0:T(8,128)(2,1)S(1)} %copy-done, bf16[256,1024]{1,0:T(8,128)(2,1)} %param.26), kind=kOutput, calls=%fused_computation.80 | convolution fusion | flops 1073741824 | bytes 9961472 | tf_op jit(solution)/shard_map/dot_general | solution.py:45
  23.4 5.9 %psum.7 = f32[16,128]{1,0:T(8,128)S(1)} all-reduce(f32[16,128]{1,0:T(8,128)S(1)} %bitcast_select_fusion.2), channel_id=1, replica_groups=mesh['ctx'=16,'shard'=2] {'shard'}, use_global_device_ids=true, to_apply=%region_10.11 | all-reduce | flops 2048 | bytes 16384 | tf_op jit(solution)/shard_map/psum | solution.py:32
  29.3 50.5 %while.53 = (s32[]{:T(128)}, bf16[256,4,128]{2,0,1:T(8,128)(2,1)S(1)}, s32[256]{0:T(256)S(1)}, f32[4,2,256]{2,1,0:T(2,128)}, f32[4,2,256]{2,1,0:T(2,128)S(1)}, /...) while((s32[]{:T(128)}, ...), condition=%wide.region_9.10_spmd.clone.clone, body=%wide.region_4.0_spmd.clone.clone.sunk | while | flops 138088976 | bytes 6874584 | solution.py:108
  30.6 4.7 %collective-permute-start.1 = (s32[256]{0:T(256)S(1)}, s32[256]{0:T(256)S(1)}, u32[]{:S(2)}, u32[]{:S(2)}) collective-permute-start(s32[256]{0:T(256)S(1)} %get-tuple-element.1321), channel_id=1, source_target_pairs={{0,2},{2,4},{4,6},{6,8},{8,10},{10,12},{12,14},{14,16},{16,18},{18... | collective-permute-start | bytes 3080 | tf_op jit(solution)/shard_map/while/body/eval_jaxpr/ppermute | solution.py:12
  38.2 5.6 %collective-permute-start = (bf16[256,4,128]{2,0,1:T(8,128)(2,1)S(1)}, bf16[256,4,128]{2,0,1:T(8,128)(2,1)S(1)}, u32[]{:S(2)}, u32[]{:S(2)}) collective-permute-start(bf16[256,4,128]{2,0,1:T(8,128)(2,1)S(1)} %get-tuple-element.1320), channel_id=1, source_target_pairs={{0,2},{2,4},{4,6},{6,8},{8,10},{10,12},{12,14},{14,16},{16,18},{18... | collective-permute-start | bytes 786440 | tf_op jit(solution)/shard_map/while/body/eval_jaxpr/ppermute | solution.py:12
  43.9 4.4 %collective-permute-start.1 = (s32[256]{0:T(256)S(1)}, s32[256]{0:T(256)S(1)}, u32[]{:S(2)}, u32[]{:S(2)}) collective-permute-start(s32[256]{0:T(256)S(1)} %get-tuple-element.1321), channel_id=1, source_target_pairs={{0,2},{2,4},{4,6},{6,8},{8,10},{10,12},{12,14},{14,16},{16,18},{18... | collective-permute-start | bytes 3080 | tf_op jit(solution)/shard_map/while/body/eval_jaxpr/ppermute | solution.py:12
  51.2 8.3 %collective-permute-start = (bf16[256,4,128]{2,0,1:T(8,128)(2,1)S(1)}, bf16[256,4,128]{2,0,1:T(8,128)(2,1)S(1)}, u32[]{:S(2)}, u32[]{:S(2)}) collective-permute-start(bf16[256,4,128]{2,0,1:T(8,128)(2,1)S(1)} %get-tuple-element.1320), channel_id=1, source_target_pairs={{0,2},{2,4},{4,6},{6,8},{8,10},{10,12},{12,14},{14,16},{16,18},{18... | collective-permute-start | bytes 786440 | tf_op jit(solution)/shard_map/while/body/eval_jaxpr/ppermute | solution.py:12
  59.5 7.5 %collective-permute-start.1 = (s32[256]{0:T(256)S(1)}, s32[256]{0:T(256)S(1)}, u32[]{:S(2)}, u32[]{:S(2)}) collective-permute-start(s32[256]{0:T(256)S(1)} %get-tuple-element.1321), channel_id=1, source_target_pairs={{0,2},{2,4},{4,6},{6,8},{8,10},{10,12},{12,14},{14,16},{16,18},{18... | collective-permute-start | bytes 3080 | tf_op jit(solution)/shard_map/while/body/eval_jaxpr/ppermute | solution.py:12
  72.4 4.4 %collective-permute-start.1 = (s32[256]{0:T(256)S(1)}, s32[256]{0:T(256)S(1)}, u32[]{:S(2)}, u32[]{:S(2)}) collective-permute-start(s32[256]{0:T(256)S(1)} %get-tuple-element.1321), channel_id=1, source_target_pairs={{0,2},{2,4},{4,6},{6,8},{8,10},{10,12},{12,14},{14,16},{16,18},{18... | collective-permute-start | bytes 3080 | tf_op jit(solution)/shard_map/while/body/eval_jaxpr/ppermute | solution.py:12
  80.5 4.4 %multiply_reduce_fusion = (f32[256,4,2]{0,2,1:T(2,128)S(1)}, bf16[1024,256]{1,0:T(8,128)(2,1)S(1)}) fusion(f32[256,1024]{0,1:T(8,128)} %copy.63, bf16[256,2048]{1,0:T(8,128)(2,1)S(1)} %copy-done, bf16[1024,2048]{1,0:T(8,128)(2,1)} %all-gather.2.cloned.1.call-done, f32[1024]{0:T(1024)S(1)} %dynamic-slice_bitcast_fusion), kind=kOutput, calls=%fused_computation.71 | convolution fusion | flops 1081079808 | bytes 6828032 | tf_op jit(solution)/shard_map/dot_general | solution.py:40
  85.1 5.4 %conditional.5 = (f32[256,4,2,128]{3,0,2,1:T(8,128)}, f32[256,4,128]{2,0,1:T(8,128)}, f32[256,4,128]{2,0,1:T(8,128)}) conditional(s32[]{:T(128)} %convert_element_type.81, () %tuple.94, (s32[]{:T(128)}, s32[256]{0:T(256)S(1)}, s32[256]{0:T(256)S(1)}, bf16[256,4,128]{0,2,1:T(8,128)(2,1)S(1)}, bf16[256,4,2,128]{0,3,2,1:T(8,128)(2,1)S(1)}, ...), branch_computations={%region_12.13_spmd, %region_13.14_spmd} | conditional | flops 675348736 | bytes 15618116 | solution.py:158
  90.5 134.6 %while.54 = (s32[]{:T(128)}, bf16[256,4,128]{2,0,1:T(8,128)(2,1)}, bf16[256,4,128]{2,0,1:T(8,128)(2,1)}, f32[256,4,2,128]{3,0,2,1:T(8,128)}, f32[256,4,128]{2,0,...) while((s32[]{:T(128)}, bf16[256,4,128]{2,0,1:T(8,128)(2,1)}, ...), condition=%wide.region_17.18_spmd.clone.clone, body=%wide.region_14.17_spmd.clone.clone.sunk | while | flops 675873280 | bytes 26111640 | solution.py:201
  96.3 4.4 %collective-permute-start.2 = (bf16[256,4,128]{2,0,1:T(8,128)(2,1)}, bf16[256,4,128]{2,0,1:T(8,128)(2,1)S(1)}, u32[]{:S(2)}, u32[]{:S(2)}) collective-permute-start(bf16[256,4,128]{2,0,1:T(8,128)(2,1)} %get-tuple-element.1370), channel_id=1, source_target_pairs={{0,2},{2,4},{4,6},{6,8},{8,10},{10,12},{12,14},{14,16},{16,18},{18... | collective-permute-start | bytes 786440 | tf_op jit(solution)/shard_map/while/body/eval_jaxpr/ppermute | solution.py:12
  105.7 7.0 %collective-permute-done.4 = f32[256,4,128]{2,0,1:T(8,128)S(1)} collective-permute-done((f32[256,4,128]{2,0,1:T(8,128)}, f32[256,4,128]{2,0,1:T(8,128)S(1)}, u32[]{:S(2)}, u32[]{:S(2)}) %collective-permute-start.4) | collective-permute-done | bytes 524320 | tf_op jit(solution)/shard_map/while/body/eval_jaxpr/ppermute | solution.py:18
  114.2 16.6 %collective-permute-start.5 = (f32[256,4,128]{2,0,1:T(8,128)}, f32[256,4,128]{2,0,1:T(8,128)S(1)}, u32[]{:S(2)}, u32[]{:S(2)}) collective-permute-start(f32[256,4,128]{2,0,1:T(8,128)} %get-tuple-element.1374), channel_id=1, source_target_pairs={{30,0},{0,2},{2,4},{4,6},{6,8},{8,10},{10,12},{12,14},{14,16},{16,... | collective-permute-start | bytes 1572872 | tf_op jit(solution)/shard_map/while/body/eval_jaxpr/ppermute | solution.py:18
  133.2 12.4 %collective-permute-start.3 = (bf16[256,4,128]{2,0,1:T(8,128)(2,1)}, bf16[256,4,128]{2,0,1:T(8,128)(2,1)}, u32[]{:S(2)}, u32[]{:S(2)}) collective-permute-start(bf16[256,4,128]{2,0,1:T(8,128)(2,1)} %get-tuple-element.1371), channel_id=1, source_target_pairs={{0,2},{2,4},{4,6},{6,8},{8,10},{10,12},{12,14},{14,16},{16,18},{18... | collective-permute-start | bytes 786440 | tf_op jit(solution)/shard_map/while/body/eval_jaxpr/ppermute | solution.py:12
  145.6 4.5 %collective-permute-start.2 = (bf16[256,4,128]{2,0,1:T(8,128)(2,1)}, bf16[256,4,128]{2,0,1:T(8,128)(2,1)S(1)}, u32[]{:S(2)}, u32[]{:S(2)}) collective-permute-start(bf16[256,4,128]{2,0,1:T(8,128)(2,1)} %get-tuple-element.1370), channel_id=1, source_target_pairs={{0,2},{2,4},{4,6},{6,8},{8,10},{10,12},{12,14},{14,16},{16,18},{18... | collective-permute-start | bytes 786440 | tf_op jit(solution)/shard_map/while/body/eval_jaxpr/ppermute | solution.py:12
  156.8 5.5 %collective-permute-start.5 = (f32[256,4,128]{2,0,1:T(8,128)}, f32[256,4,128]{2,0,1:T(8,128)S(1)}, u32[]{:S(2)}, u32[]{:S(2)}) collective-permute-start(f32[256,4,128]{2,0,1:T(8,128)} %get-tuple-element.1374), channel_id=1, source_target_pairs={{30,0},{0,2},{2,4},{4,6},{6,8},{8,10},{10,12},{12,14},{14,16},{16,... | collective-permute-start | bytes 1572872 | tf_op jit(solution)/shard_map/while/body/eval_jaxpr/ppermute | solution.py:18
  162.2 8.3 %collective-permute-start.4 = (f32[256,4,128]{2,0,1:T(8,128)}, f32[256,4,128]{2,0,1:T(8,128)S(1)}, u32[]{:S(2)}, u32[]{:S(2)}) collective-permute-start(f32[256,4,128]{2,0,1:T(8,128)} %get-tuple-element.1373), channel_id=1, source_target_pairs={{30,0},{0,2},{2,4},{4,6},{6,8},{8,10},{10,12},{12,14},{14,16},{16,... | collective-permute-start | bytes 1572872 | tf_op jit(solution)/shard_map/while/body/eval_jaxpr/ppermute | solution.py:18
  173.1 4.2 %collective-permute-start.2 = (bf16[256,4,128]{2,0,1:T(8,128)(2,1)}, bf16[256,4,128]{2,0,1:T(8,128)(2,1)S(1)}, u32[]{:S(2)}, u32[]{:S(2)}) collective-permute-start(bf16[256,4,128]{2,0,1:T(8,128)(2,1)} %get-tuple-element.1370), channel_id=1, source_target_pairs={{0,2},{2,4},{4,6},{6,8},{8,10},{10,12},{12,14},{14,16},{16,18},{18... | collective-permute-start | bytes 786440 | tf_op jit(solution)/shard_map/while/body/eval_jaxpr/ppermute | solution.py:12
  183.9 12.2 %collective-permute-start.5 = (f32[256,4,128]{2,0,1:T(8,128)}, f32[256,4,128]{2,0,1:T(8,128)S(1)}, u32[]{:S(2)}, u32[]{:S(2)}) collective-permute-start(f32[256,4,128]{2,0,1:T(8,128)} %get-tuple-element.1374), channel_id=1, source_target_pairs={{30,0},{0,2},{2,4},{4,6},{6,8},{8,10},{10,12},{12,14},{14,16},{16,... | collective-permute-start | bytes 1572872 | tf_op jit(solution)/shard_map/while/body/eval_jaxpr/ppermute | solution.py:18
  198.5 15.5 %collective-permute-start.3 = (bf16[256,4,128]{2,0,1:T(8,128)(2,1)}, bf16[256,4,128]{2,0,1:T(8,128)(2,1)}, u32[]{:S(2)}, u32[]{:S(2)}) collective-permute-start(bf16[256,4,128]{2,0,1:T(8,128)(2,1)} %get-tuple-element.1371), channel_id=1, source_target_pairs={{0,2},{2,4},{4,6},{6,8},{8,10},{10,12},{12,14},{14,16},{16,18},{18... | collective-permute-start | bytes 786440 | tf_op jit(solution)/shard_map/while/body/eval_jaxpr/ppermute | solution.py:12
  214.1 4.5 %collective-permute-start.2 = (bf16[256,4,128]{2,0,1:T(8,128)(2,1)}, bf16[256,4,128]{2,0,1:T(8,128)(2,1)S(1)}, u32[]{:S(2)}, u32[]{:S(2)}) collective-permute-start(bf16[256,4,128]{2,0,1:T(8,128)(2,1)} %get-tuple-element.1370), channel_id=1, source_target_pairs={{0,2},{2,4},{4,6},{6,8},{8,10},{10,12},{12,14},{14,16},{16,18},{18... | collective-permute-start | bytes 786440 | tf_op jit(solution)/shard_map/while/body/eval_jaxpr/ppermute | solution.py:12
  226.2 27.4 %collective-permute-start.7 = (bf16[256,4,128]{2,0,1:T(8,128)(2,1)S(1)}, bf16[256,4,128]{2,0,1:T(8,128)(2,1)S(1)}, u32[]{:S(2)}, u32[]{:S(2)}) collective-permute-start(bf16[256,4,128]{2,0,1:T(8,128)(2,1)S(1)} %convert_element_type.93), channel_id=1, source_target_pairs={{8,0},{10,2},{12,4},{14,6},{16,8},{18,10},{20,12},{22,14},{24,16},... | collective-permute-start | bytes 786440 | tf_op jit(solution)/shard_map/ppermute | solution.py:18
  (166 shorter events, 72.9 us)
Async XLA Ops:
  7.2 73.3 %all-gather.2.cloned.1.call-start = ((), (), s32[]{:S(2)}) async-start(), calls=%async_computation.1 | async-start | bytes 4456448 | tf_op jit(solution)/shard_map/all_gather | solution.py:37
  7.9 254.0 %reduce-scatter.2.cloned.1.call-start = ((), (), s32[]{:S(2)}) async-start(), calls=%async_computation.2 | async-start | bytes 8912896 | tf_op jit(solution)/shard_map/reduce_scatter | solution.py:44
  29.3 8.8 %collective-permute-start = (bf16[256,4,128]{2,0,1:T(8,128)(2,1)S(1)}, bf16[256,4,128]{2,0,1:T(8,128)(2,1)S(1)}, u32[]{:S(2)}, u32[]{:S(2)}) collective-permute-start(bf16[256,4,128]{2,0,1:T(8,128)(2,1)S(1)} %get-tuple-element.1320), channel_id=1, source_target_pairs={{0,2},{2,4},{4,6},{6,8},{8,10},{10,12},{12,14},{14,16},{16,18},{18... | collective-permute-start | bytes 786440 | tf_op jit(solution)/shard_map/while/body/eval_jaxpr/ppermute | solution.py:12
  38.2 12.9 %collective-permute-start = (bf16[256,4,128]{2,0,1:T(8,128)(2,1)S(1)}, bf16[256,4,128]{2,0,1:T(8,128)(2,1)S(1)}, u32[]{:S(2)}, u32[]{:S(2)}) collective-permute-start(bf16[256,4,128]{2,0,1:T(8,128)(2,1)S(1)} %get-tuple-element.1320), channel_id=1, source_target_pairs={{0,2},{2,4},{4,6},{6,8},{8,10},{10,12},{12,14},{14,16},{16,18},{18... | collective-permute-start | bytes 786440 | tf_op jit(solution)/shard_map/while/body/eval_jaxpr/ppermute | solution.py:12
  51.2 18.6 %collective-permute-start = (bf16[256,4,128]{2,0,1:T(8,128)(2,1)S(1)}, bf16[256,4,128]{2,0,1:T(8,128)(2,1)S(1)}, u32[]{:S(2)}, u32[]{:S(2)}) collective-permute-start(bf16[256,4,128]{2,0,1:T(8,128)(2,1)S(1)} %get-tuple-element.1320), channel_id=1, source_target_pairs={{0,2},{2,4},{4,6},{6,8},{8,10},{10,12},{12,14},{14,16},{16,18},{18... | collective-permute-start | bytes 786440 | tf_op jit(solution)/shard_map/while/body/eval_jaxpr/ppermute | solution.py:12
  59.5 8.3 %collective-permute-start.1 = (s32[256]{0:T(256)S(1)}, s32[256]{0:T(256)S(1)}, u32[]{:S(2)}, u32[]{:S(2)}) collective-permute-start(s32[256]{0:T(256)S(1)} %get-tuple-element.1321), channel_id=1, source_target_pairs={{0,2},{2,4},{4,6},{6,8},{8,10},{10,12},{12,14},{14,16},{16,18},{18... | collective-permute-start | bytes 3080 | tf_op jit(solution)/shard_map/while/body/eval_jaxpr/ppermute | solution.py:12
  69.9 9.8 %collective-permute-start = (bf16[256,4,128]{2,0,1:T(8,128)(2,1)S(1)}, bf16[256,4,128]{2,0,1:T(8,128)(2,1)S(1)}, u32[]{:S(2)}, u32[]{:S(2)}) collective-permute-start(bf16[256,4,128]{2,0,1:T(8,128)(2,1)S(1)} %get-tuple-element.1320), channel_id=1, source_target_pairs={{0,2},{2,4},{4,6},{6,8},{8,10},{10,12},{12,14},{14,16},{16,18},{18... | collective-permute-start | bytes 786440 | tf_op jit(solution)/shard_map/while/body/eval_jaxpr/ppermute | solution.py:12
  90.5 15.1 %collective-permute-start.5 = (f32[256,4,128]{2,0,1:T(8,128)}, f32[256,4,128]{2,0,1:T(8,128)S(1)}, u32[]{:S(2)}, u32[]{:S(2)}) collective-permute-start(f32[256,4,128]{2,0,1:T(8,128)} %get-tuple-element.1374), channel_id=1, source_target_pairs={{30,0},{0,2},{2,4},{4,6},{6,8},{8,10},{10,12},{12,14},{14,16},{16,... | collective-permute-start | bytes 1572872 | tf_op jit(solution)/shard_map/while/body/eval_jaxpr/ppermute | solution.py:18
  91.1 21.5 %collective-permute-start.4 = (f32[256,4,128]{2,0,1:T(8,128)}, f32[256,4,128]{2,0,1:T(8,128)S(1)}, u32[]{:S(2)}, u32[]{:S(2)}) collective-permute-start(f32[256,4,128]{2,0,1:T(8,128)} %get-tuple-element.1373), channel_id=1, source_target_pairs={{30,0},{0,2},{2,4},{4,6},{6,8},{8,10},{10,12},{12,14},{14,16},{16,... | collective-permute-start | bytes 1572872 | tf_op jit(solution)/shard_map/while/body/eval_jaxpr/ppermute | solution.py:18
  93.6 9.6 %collective-permute-start.3 = (bf16[256,4,128]{2,0,1:T(8,128)(2,1)}, bf16[256,4,128]{2,0,1:T(8,128)(2,1)}, u32[]{:S(2)}, u32[]{:S(2)}) collective-permute-start(bf16[256,4,128]{2,0,1:T(8,128)(2,1)} %get-tuple-element.1371), channel_id=1, source_target_pairs={{0,2},{2,4},{4,6},{6,8},{8,10},{10,12},{12,14},{14,16},{16,18},{18... | collective-permute-start | bytes 786440 | tf_op jit(solution)/shard_map/while/body/eval_jaxpr/ppermute | solution.py:12
  96.3 8.7 %collective-permute-start.2 = (bf16[256,4,128]{2,0,1:T(8,128)(2,1)}, bf16[256,4,128]{2,0,1:T(8,128)(2,1)S(1)}, u32[]{:S(2)}, u32[]{:S(2)}) collective-permute-start(bf16[256,4,128]{2,0,1:T(8,128)(2,1)} %get-tuple-element.1370), channel_id=1, source_target_pairs={{0,2},{2,4},{4,6},{6,8},{8,10},{10,12},{12,14},{14,16},{16,18},{18... | collective-permute-start | bytes 786440 | tf_op jit(solution)/shard_map/while/body/eval_jaxpr/ppermute | solution.py:12
  114.2 40.9 %collective-permute-start.5 = (f32[256,4,128]{2,0,1:T(8,128)}, f32[256,4,128]{2,0,1:T(8,128)S(1)}, u32[]{:S(2)}, u32[]{:S(2)}) collective-permute-start(f32[256,4,128]{2,0,1:T(8,128)} %get-tuple-element.1374), channel_id=1, source_target_pairs={{30,0},{0,2},{2,4},{4,6},{6,8},{8,10},{10,12},{12,14},{14,16},{16,... | collective-permute-start | bytes 1572872 | tf_op jit(solution)/shard_map/while/body/eval_jaxpr/ppermute | solution.py:18
  130.8 24.3 %collective-permute-start.4 = (f32[256,4,128]{2,0,1:T(8,128)}, f32[256,4,128]{2,0,1:T(8,128)S(1)}, u32[]{:S(2)}, u32[]{:S(2)}) collective-permute-start(f32[256,4,128]{2,0,1:T(8,128)} %get-tuple-element.1373), channel_id=1, source_target_pairs={{30,0},{0,2},{2,4},{4,6},{6,8},{8,10},{10,12},{12,14},{14,16},{16,... | collective-permute-start | bytes 1572872 | tf_op jit(solution)/shard_map/while/body/eval_jaxpr/ppermute | solution.py:18
  133.2 19.5 %collective-permute-start.3 = (bf16[256,4,128]{2,0,1:T(8,128)(2,1)}, bf16[256,4,128]{2,0,1:T(8,128)(2,1)}, u32[]{:S(2)}, u32[]{:S(2)}) collective-permute-start(bf16[256,4,128]{2,0,1:T(8,128)(2,1)} %get-tuple-element.1371), channel_id=1, source_target_pairs={{0,2},{2,4},{4,6},{6,8},{8,10},{10,12},{12,14},{14,16},{16,18},{18... | collective-permute-start | bytes 786440 | tf_op jit(solution)/shard_map/while/body/eval_jaxpr/ppermute | solution.py:12
  145.6 8.8 %collective-permute-start.2 = (bf16[256,4,128]{2,0,1:T(8,128)(2,1)}, bf16[256,4,128]{2,0,1:T(8,128)(2,1)S(1)}, u32[]{:S(2)}, u32[]{:S(2)}) collective-permute-start(bf16[256,4,128]{2,0,1:T(8,128)(2,1)} %get-tuple-element.1370), channel_id=1, source_target_pairs={{0,2},{2,4},{4,6},{6,8},{8,10},{10,12},{12,14},{14,16},{16,18},{18... | collective-permute-start | bytes 786440 | tf_op jit(solution)/shard_map/while/body/eval_jaxpr/ppermute | solution.py:12
  156.8 25.5 %collective-permute-start.5 = (f32[256,4,128]{2,0,1:T(8,128)}, f32[256,4,128]{2,0,1:T(8,128)S(1)}, u32[]{:S(2)}, u32[]{:S(2)}) collective-permute-start(f32[256,4,128]{2,0,1:T(8,128)} %get-tuple-element.1374), channel_id=1, source_target_pairs={{30,0},{0,2},{2,4},{4,6},{6,8},{8,10},{10,12},{12,14},{14,16},{16,... | collective-permute-start | bytes 1572872 | tf_op jit(solution)/shard_map/while/body/eval_jaxpr/ppermute | solution.py:18
  162.2 20.1 %collective-permute-start.4 = (f32[256,4,128]{2,0,1:T(8,128)}, f32[256,4,128]{2,0,1:T(8,128)S(1)}, u32[]{:S(2)}, u32[]{:S(2)}) collective-permute-start(f32[256,4,128]{2,0,1:T(8,128)} %get-tuple-element.1373), channel_id=1, source_target_pairs={{30,0},{0,2},{2,4},{4,6},{6,8},{8,10},{10,12},{12,14},{14,16},{16,... | collective-permute-start | bytes 1572872 | tf_op jit(solution)/shard_map/while/body/eval_jaxpr/ppermute | solution.py:18
  170.5 9.4 %collective-permute-start.3 = (bf16[256,4,128]{2,0,1:T(8,128)(2,1)}, bf16[256,4,128]{2,0,1:T(8,128)(2,1)}, u32[]{:S(2)}, u32[]{:S(2)}) collective-permute-start(bf16[256,4,128]{2,0,1:T(8,128)(2,1)} %get-tuple-element.1371), channel_id=1, source_target_pairs={{0,2},{2,4},{4,6},{6,8},{8,10},{10,12},{12,14},{14,16},{16,18},{18... | collective-permute-start | bytes 786440 | tf_op jit(solution)/shard_map/while/body/eval_jaxpr/ppermute | solution.py:12
  173.1 8.4 %collective-permute-start.2 = (bf16[256,4,128]{2,0,1:T(8,128)(2,1)}, bf16[256,4,128]{2,0,1:T(8,128)(2,1)S(1)}, u32[]{:S(2)}, u32[]{:S(2)}) collective-permute-start(bf16[256,4,128]{2,0,1:T(8,128)(2,1)} %get-tuple-element.1370), channel_id=1, source_target_pairs={{0,2},{2,4},{4,6},{6,8},{8,10},{10,12},{12,14},{14,16},{16,18},{18... | collective-permute-start | bytes 786440 | tf_op jit(solution)/shard_map/while/body/eval_jaxpr/ppermute | solution.py:12
  183.9 39.6 %collective-permute-start.5 = (f32[256,4,128]{2,0,1:T(8,128)}, f32[256,4,128]{2,0,1:T(8,128)S(1)}, u32[]{:S(2)}, u32[]{:S(2)}) collective-permute-start(f32[256,4,128]{2,0,1:T(8,128)} %get-tuple-element.1374), channel_id=1, source_target_pairs={{30,0},{0,2},{2,4},{4,6},{6,8},{8,10},{10,12},{12,14},{14,16},{16,... | collective-permute-start | bytes 1572872 | tf_op jit(solution)/shard_map/while/body/eval_jaxpr/ppermute | solution.py:18
  196.1 27.4 %collective-permute-start.4 = (f32[256,4,128]{2,0,1:T(8,128)}, f32[256,4,128]{2,0,1:T(8,128)S(1)}, u32[]{:S(2)}, u32[]{:S(2)}) collective-permute-start(f32[256,4,128]{2,0,1:T(8,128)} %get-tuple-element.1373), channel_id=1, source_target_pairs={{30,0},{0,2},{2,4},{4,6},{6,8},{8,10},{10,12},{12,14},{14,16},{16,... | collective-permute-start | bytes 1572872 | tf_op jit(solution)/shard_map/while/body/eval_jaxpr/ppermute | solution.py:18
  198.5 22.6 %collective-permute-start.3 = (bf16[256,4,128]{2,0,1:T(8,128)(2,1)}, bf16[256,4,128]{2,0,1:T(8,128)(2,1)}, u32[]{:S(2)}, u32[]{:S(2)}) collective-permute-start(bf16[256,4,128]{2,0,1:T(8,128)(2,1)} %get-tuple-element.1371), channel_id=1, source_target_pairs={{0,2},{2,4},{4,6},{6,8},{8,10},{10,12},{12,14},{14,16},{16,18},{18... | collective-permute-start | bytes 786440 | tf_op jit(solution)/shard_map/while/body/eval_jaxpr/ppermute | solution.py:12
  214.1 8.8 %collective-permute-start.2 = (bf16[256,4,128]{2,0,1:T(8,128)(2,1)}, bf16[256,4,128]{2,0,1:T(8,128)(2,1)S(1)}, u32[]{:S(2)}, u32[]{:S(2)}) collective-permute-start(bf16[256,4,128]{2,0,1:T(8,128)(2,1)} %get-tuple-element.1370), channel_id=1, source_target_pairs={{0,2},{2,4},{4,6},{6,8},{8,10},{10,12},{12,14},{14,16},{16,18},{18... | collective-permute-start | bytes 786440 | tf_op jit(solution)/shard_map/while/body/eval_jaxpr/ppermute | solution.py:12
  226.2 32.1 %collective-permute-start.7 = (bf16[256,4,128]{2,0,1:T(8,128)(2,1)S(1)}, bf16[256,4,128]{2,0,1:T(8,128)(2,1)S(1)}, u32[]{:S(2)}, u32[]{:S(2)}) collective-permute-start(bf16[256,4,128]{2,0,1:T(8,128)(2,1)S(1)} %convert_element_type.93), channel_id=1, source_target_pairs={{8,0},{10,2},{12,4},{14,6},{16,8},{18,10},{20,12},{22,14},{24,16},... | collective-permute-start | bytes 786440 | tf_op jit(solution)/shard_map/ppermute | solution.py:18
  (15 other events, 49.6 us)
Sparse Core Ops, SparseCore 0:
  10.1 57.1 all-gather.1
  71.4 129.0 reduce-scatter.1
where the time goes:
time: 272 us; the launch traced here: 271 us
  starting transfers between devices  168 us (62%)
  local copies, waits for them, and re-layouts  35.1 us (13%)
  matrix products  15.7 us (6%)
  between operations  15.5 us (6%)
  loops' own time  11.5 us (4%)
  waiting for transfers between devices  10.6 us (4%)
  other arithmetic  8.2 us (3%)
  blocking collectives  5.91 us (2%)
    ppermute x16, starting transfers between devices, from_behind(): return lax.ppermute(x, axis, pairs)  89.6 us
    ppermute x10, starting transfers between devices, shifted(): return lax.ppermute(block, axis, route)  78.5 us
    while x24, local copies, waits for them, and re-layouts  15.9 us
    ppermute x10, waiting for transfers between devices, shifted(): return lax.ppermute(block, axis, route)  9.05 us
    psum x1, blocking collectives, per_device(): scale_table = lax.psum(jnp.where(owned, scale_copies[0], 0.0), 'shard')  5.91 us
    another operation x1, loops' own time, per_device(): lax.fori_loop(1, cycle_steps, stats_step, (head_keys, doc_ids, softmax_st...  5.7 us
    dot_general x1, matrix products, per_device(): lax.dot_general(columns, attention_output, (((0,), (0,)), ((), ())), pref...  5.58 us
    another operation x1, loops' own time, per_device(): lax.fori_loop(1, cycle_steps, keys_step, (head_keys, head_values, own_sum...  5.55 us
  transfers between devices with their start and end apart: 28, of which 6 were waited for; matrix products, arithmetic and copies ran while one was open for 20% of the time, Pallas kernels for 0%

commit v1 on v0

v1 whole, which is shorter than its diff:
```python
import functools
import jax
import jax.numpy as jnp
from jax import lax
from jax.experimental import pallas as pl
from jax.sharding import PartitionSpec as P

HEAD_WIDTH = 128
LOW = -1e30
LAST = (((1,), (1,)), ((), ()))
FIRST = (((0,), (0,)), ((), ()))
PLAIN = (((1,), (0,)), ((), ()))


def dot(a, b, dims):
    return lax.dot_general(a, b, dims, preferred_element_type=jnp.float32)


def stacked(ref, pairs):
    return jnp.concatenate(
        [ref[:, j * HEAD_WIDTH : (j + 1) * HEAD_WIDTH] for j in range(pairs)], axis=0
    )


def row_of(ref, pairs):
    return jnp.concatenate([ref[0, j : j + 1, :] for j in range(pairs)], axis=1)


def visible(key_docs_ref, query_docs_ref, pairs, own):
    key_docs = key_docs_ref[:, 0:1].astype(jnp.float32)
    query_docs = query_docs_ref[...]
    allowed = key_docs == query_docs
    if own:
        rows = query_docs.shape[1]
        n = lax.broadcasted_iota(jnp.int32, (rows, rows), 0)
        r = lax.broadcasted_iota(jnp.int32, (rows, rows), 1)
        allowed = allowed & (n <= r)
    return jnp.concatenate([allowed.astype(jnp.float32)] * pairs, axis=1) > 0.5


def stats_kernel(own, final, pairs, scale, q_ref, k_ref, kd_ref, qd_ref, m_ref, l_ref, *outs):
    rows = q_ref.shape[0]
    scores = dot(k_ref[...], stacked(q_ref, pairs), LAST) * scale
    allowed = visible(kd_ref, qd_ref, pairs, own)
    masked = jnp.where(allowed, scores, LOW)
    highest, running = row_of(m_ref, pairs), row_of(l_ref, pairs)
    newest = jnp.maximum(highest, jnp.max(masked, axis=0, keepdims=True))
    weights = jnp.where(allowed, jnp.exp(scores - newest), 0.0)
    total = running * jnp.exp(highest - newest) + jnp.sum(weights, axis=0, keepdims=True)
    results = (newest + jnp.log(total),) if final else (newest, total)
    for out, result in zip(outs, results):
        for j in range(pairs):
            out[0, j : j + 1, :] = result[:, j * rows : (j + 1) * rows]


def grads_kernel(
    own, first, pairs, scale, q_ref, a_ref, k_ref, v_ref, kd_ref, qd_ref, t_ref, d_ref, *rest
):
    if first:
        dq_ref, kv_ref = rest
    else:
        old_ref, dq_ref, kv_ref = rest
    rows = q_ref.shape[0]
    queries, grads = stacked(q_ref, pairs), stacked(a_ref, pairs)
    keys, values = k_ref[...], v_ref[...]
    scores = dot(keys, queries, LAST) * scale
    allowed = visible(kd_ref, qd_ref, pairs, own)
    attention = jnp.where(allowed, jnp.exp(scores - row_of(t_ref, pairs)), 0.0)
    attention_grad = dot(values, grads, LAST)
    score_grad = (attention * (attention_grad - row_of(d_ref, pairs))).astype(jnp.bfloat16)
    kv_ref[0] = (dot(score_grad, queries, PLAIN) * scale).astype(kv_ref.dtype)
    kv_ref[1] = dot(attention.astype(jnp.bfloat16), grads, PLAIN).astype(kv_ref.dtype)
    query_add = dot(score_grad, keys, FIRST) * scale
    for j in range(pairs):
        part = query_add[j * rows : (j + 1) * rows, :]
        cols = slice(j * HEAD_WIDTH, (j + 1) * HEAD_WIDTH)
        if not first:
            part = part + old_ref[:, cols]
        dq_ref[:, cols] = part.astype(dq_ref.dtype)


def shift_by(x, axis, by):
    size = lax.axis_size(axis)
    return lax.ppermute(x, axis, [(i, i + by) for i in range(size) if 0 <= i + by < size])


def per_device(query, key, value, attention_output, grad_y, doc_ids, codes, scale_copies, holder):
    rows = query.shape[0]
    heads = query.shape[1] // HEAD_WIDTH
    groups = key.shape[1] // HEAD_WIDTH
    pairs = heads // groups
    shard_index = lax.axis_index("shard")
    shards = lax.axis_size("shard")
    ctx_count = lax.axis_size("ctx")
    steps = ctx_count // 4 + 1
    scale = HEAD_WIDTH ** (-0.5)

    gathered = lax.all_gather(codes, "ctx", axis=1, tiled=True)

    docs = (doc_ids + 1).astype(jnp.bfloat16)
    packed = jnp.concatenate(
        [key, value, jnp.broadcast_to(docs[:, None], (rows, HEAD_WIDTH))], axis=1
    )
    query_docs = (doc_ids + 1).astype(jnp.float32)[None, :]
    blocks = [packed] + [shift_by(packed, "ctx", d) for d in range(1, steps)]

    masked_table = jnp.where((holder == shard_index)[:, None], scale_copies[0], 0.0)
    scale_table = masked_table
    for i in range(1, shards):
        scale_table = scale_table + lax.ppermute(
            masked_table, "shard", [(j, (j + i) % shards) for j in range(shards)]
        )
    row_scale = lax.dynamic_slice_in_dim(scale_table, shard_index * heads, heads, 0).reshape(
        heads * HEAD_WIDTH
    )

    partial_weight = (
        dot(grad_y, attention_output, FIRST) * (rows * ctx_count) ** (-0.5)
    ).astype(jnp.bfloat16)
    scattered = lax.psum_scatter(partial_weight, "ctx", scatter_dimension=0, tiled=True)

    pair_spec = pl.BlockSpec((rows, pairs * HEAD_WIDTH), lambda g: (0, g))
    key_spec = pl.BlockSpec((rows, HEAD_WIDTH), lambda g: (0, g))
    value_spec = pl.BlockSpec((rows, HEAD_WIDTH), lambda g: (0, groups + g))
    docs_spec = pl.BlockSpec((rows, HEAD_WIDTH), lambda g: (0, 2 * groups))
    query_docs_spec = pl.BlockSpec((1, rows), lambda g: (0, 0))
    row_spec = pl.BlockSpec((1, pairs, rows), lambda g: (g, 0, 0))
    row_shape = jax.ShapeDtypeStruct((groups, pairs, rows), jnp.float32)
    tile = 2 * rows * rows * HEAD_WIDTH * heads

    def stats(block, state, own, final):
        count = 1 if final else 2
        return pl.pallas_call(
            functools.partial(stats_kernel, own, final, pairs, scale),
            grid=(groups,),
            in_specs=[pair_spec, key_spec, docs_spec, query_docs_spec, row_spec, row_spec],
            out_specs=[row_spec] * count,
            out_shape=[row_shape] * count,
            cost_estimate=pl.CostEstimate(
                flops=2 * tile, bytes_accessed=1 << 20, transcendentals=rows * rows * heads
            ),
            name="stats",
        )(query, block, block, query_docs, *state)

    state = [jnp.full(row_shape.shape, LOW, jnp.float32), jnp.zeros(row_shape.shape, jnp.float32)]
    for d in range(steps):
        state = stats(blocks[d], state, d == 0, d == steps - 1)
    log_total = state[0]

    weight = (gathered.astype(jnp.float32) * row_scale[:, None]).astype(jnp.bfloat16)
    attention_gradient = dot(grad_y, weight, LAST).astype(jnp.bfloat16)
    row_delta = jnp.sum(
        attention_gradient.reshape(rows, groups, pairs, HEAD_WIDTH).astype(jnp.float32)
        * attention_output.reshape(rows, groups, pairs, HEAD_WIDTH).astype(jnp.float32),
        axis=-1,
    ).transpose(1, 2, 0)

    def grads(block, total, own):
        first = total is None
        wide = jnp.float32 if own else jnp.bfloat16
        key_shape = jax.ShapeDtypeStruct((2, rows, groups * HEAD_WIDTH), wide)
        both_spec = pl.BlockSpec((2, rows, HEAD_WIDTH), lambda g: (0, 0, g))
        ins = [pair_spec, pair_spec, key_spec, value_spec, docs_spec, query_docs_spec]
        return pl.pallas_call(
            functools.partial(grads_kernel, own, first, pairs, scale),
            grid=(groups,),
            in_specs=ins + [row_spec, row_spec] + ([] if first else [pair_spec]),
            out_specs=[pair_spec, both_spec],
            out_shape=[
                jax.ShapeDtypeStruct(query.shape, jnp.bfloat16 if own else jnp.float32),
                key_shape,
            ],
            cost_estimate=pl.CostEstimate(
                flops=10 * tile, bytes_accessed=4 << 20, transcendentals=rows * rows * heads
            ),
            name="grads",
        )(
            query,
            attention_gradient,
            block,
            block,
            block,
            query_docs,
            log_total,
            row_delta,
            *([] if first else [total]),
        )

    total = None
    parts = []
    for d in reversed(range(steps)):
        total, part = grads(blocks[d], total, d == 0)
        if d:
            part = shift_by(part, "ctx", -d)
        parts.append(part)
    summed = sum(part.astype(jnp.float32) for part in parts).astype(jnp.bfloat16)
    key_gradient, value_gradient = summed[0], summed[1]
    grad_weight = scattered.astype(jnp.float32)
    return (total, key_gradient, value_gradient, grad_weight)


def solution(mesh):
    return jax.shard_map(
        per_device,
        mesh=mesh,
        in_specs=(
            P("ctx", "shard"),
            P("ctx", "shard"),
            P("ctx", "shard"),
            P("ctx", "shard"),
            P("ctx", None),
            P("ctx"),
            P("shard", "ctx"),
            P("shard", None, None),
            P(),
        ),
        out_specs=(P("ctx", "shard"), P("ctx", "shard"), P("ctx", "shard"), P("ctx", "shard")),
        check_vma=False,
    )
```

time: 272 us -> 196 us (0.72)
  starting transfers between devices: 168 us -> 21.5 us
  waiting for transfers between devices: 10.6 us -> 93.1 us
  Pallas kernels: 0 us -> 45.4 us
  local copies, waits for them, and re-layouts: 35.1 us -> 6.53 us
  loops' own time: 11.5 us -> 0 us
  matrix products: 15.7 us -> 8.66 us
  blocking collectives: 5.91 us -> 0 us
    ppermute x26 -> x9, starting transfers between devices: 168 us -> 21.4 us  [the longest x8 19.9 us: shift_by(): lax.ppermute(x, axis, [(i, i + by) for i in range(size) if 0 <= i + by <...]
    reduce_scatter x1, waiting for transfers between devices: 0.01 us -> 66.1 us  [per_device(): lax.psum_scatter(partial_weight, 'ctx', scatter_dimension=0, tiled=True)]
    pallas_call x0 -> x10, Pallas kernels: none -> 45.4 us  [the longest x5 25.8 us: grads(): pl.pallas_call(functools.partial(grads_kernel, own, first, pairs, scale),...]
    all_gather x1, waiting for transfers between devices: 0.01 us -> 21.7 us  [per_device(): gathered = lax.all_gather(codes, 'ctx', axis=1, tiled=True)]
    while x24 -> x0, local copies, waits for them, and re-layouts: 15.9 us -> none
    another operation x12 -> x0, loops' own time: 11.5 us -> none  [the longest x1 5.7 us: per_device(): lax.fori_loop(1, cycle_steps, stats_step, (head_keys, doc_ids, softmax_st...]
    slice x17 -> x0, local copies, waits for them, and re-layouts: 10.3 us -> none  [the longest x9 5.3 us: is_live(): query_docs[0]]
    dot_general x8 -> x2, matrix products: 15.7 us -> 8.66 us  [dot(): return lax.dot_general(a, b, dims, preferred_element_type=jnp.float32)]
  transfers between devices with their start and end apart: 28 -> 11, of which waited for: 6 -> 4; matrix products, arithmetic and copies ran while one was open for 20% -> 8% of each run, Pallas kernels for 0% -> 23%
where the time goes in v1:
time: 196 us; the launch traced here: 195 us
  waiting for transfers between devices  93.1 us (48%)
  Pallas kernels  45.4 us (23%)
  starting transfers between devices  21.5 us (11%)
  between operations  14.3 us (7%)
  matrix products  8.66 us (4%)
  local copies, waits for them, and re-layouts  6.53 us (3%)
  other arithmetic  5.6 us (3%)
    reduce_scatter x1, waiting for transfers between devices, per_device(): lax.psum_scatter(partial_weight, 'ctx', scatter_dimension=0, tiled=True)  66.1 us
    pallas_call x5, Pallas kernels, grads(): pl.pallas_call(functools.partial(grads_kernel, own, first, pairs, scale),...  25.8 us
    all_gather x1, waiting for transfers between devices, per_device(): gathered = lax.all_gather(codes, 'ctx', axis=1, tiled=True)  21.7 us
    ppermute x8, starting transfers between devices, shift_by(): lax.ppermute(x, axis, [(i, i + by) for i in range(size) if 0 <= i + by <...  19.9 us
    pallas_call x5, Pallas kernels, stats(): pl.pallas_call(functools.partial(stats_kernel, own, final, pairs, scale),...  19.6 us
    dot_general x2, matrix products, dot(): return lax.dot_general(a, b, dims, preferred_element_type=jnp.float32)  8.66 us
    ppermute x8, waiting for transfers between devices, shift_by(): lax.ppermute(x, axis, [(i, i + by) for i in range(size) if 0 <= i + by <...  4.54 us
  transfers between devices with their start and end apart: 11, of which 4 were waited for; matrix products, arithmetic and copies ran while one was open for 8% of the time, Pallas kernels for 23%

profile of v1, /device:TPU:0, one launch (start us, length us, event | category | flops | bytes accessed | tf_op | source)
XLA Modules:
  0.0 195.0 jit_solution(9859182587229395828)
XLA Ops:
  8.4 4.3 %multiply_convert_fusion = bf16[2048,1024]{1,0:T(8,128)(2,1)} fusion(bf16[256,2048]{1,0:T(8,128)(2,1)S(1)} %copy-done, bf16[256,1024]{1,0:T(8,128)(2,1)} %param.12), kind=kOutput, calls=%fused_computation | convolution fusion | flops 1077936128 | bytes 5767168 | tf_op jit(solution)/shard_map/dot_general | solution.py:16
  14.1 2.4 %collective-permute-start.4 = (bf16[256,1152]{1,0:T(8,128)(2,1)S(1)}, bf16[256,1152]{1,0:T(8,128)(2,1)S(1)}, u32[]{:S(2)}, u32[]{:S(2)}) collective-permute-start(bf16[256,1152]{1,0:T(8,128)(2,1)S(1)} %pad_maximum_fusion.k_ref.kd_ref.v_ref), channel_id=1, source_target_pairs={{0,2},{2,4},{4,6},{6,8},{8,10},{10,12},{12,14},{14,16},{16,18},{18... | collective-permute-start | bytes 1769480 | tf_op jit(solution)/shard_map/ppermute | solution.py:84
  16.5 5.2 %collective-permute-start.3 = (bf16[256,1152]{1,0:T(8,128)(2,1)S(1)}, bf16[256,1152]{1,0:T(8,128)(2,1)}, u32[]{:S(2)}, u32[]{:S(2)}) collective-permute-start(bf16[256,1152]{1,0:T(8,128)(2,1)S(1)} %pad_maximum_fusion.k_ref.kd_ref.v_ref), channel_id=1, source_target_pairs={{0,4},{2,6},{4,8},{6,10},{8,12},{10,14},{12,16},{14,18},{16,20},{1... | collective-permute-start | bytes 1769480 | tf_op jit(solution)/shard_map/ppermute | solution.py:84
  21.8 4.4 %collective-permute-start.2 = (bf16[256,1152]{1,0:T(8,128)(2,1)S(1)}, bf16[256,1152]{1,0:T(8,128)(2,1)}, u32[]{:S(2)}, u32[]{:S(2)}) collective-permute-start(bf16[256,1152]{1,0:T(8,128)(2,1)S(1)} %pad_maximum_fusion.k_ref.kd_ref.v_ref), channel_id=1, source_target_pairs={{0,6},{2,8},{4,10},{6,12},{8,14},{10,16},{12,18},{14,20},{16,22},{... | collective-permute-start | bytes 1769480 | tf_op jit(solution)/shard_map/ppermute | solution.py:84
  26.1 2.7 %collective-permute-start.1 = (bf16[256,1152]{1,0:T(8,128)(2,1)S(1)}, bf16[256,1152]{1,0:T(8,128)(2,1)S(1)}, u32[]{:S(2)}, u32[]{:S(2)}) collective-permute-start(bf16[256,1152]{1,0:T(8,128)(2,1)S(1)} %pad_maximum_fusion.k_ref.kd_ref.v_ref), channel_id=1, source_target_pairs={{0,8},{2,10},{4,12},{6,14},{8,16},{10,18},{12,20},{14,22},{16,24},... | collective-permute-start | bytes 1769480 | tf_op jit(solution)/shard_map/ppermute | solution.py:84
  29.0 1.5 collective-permute-start
  31.7 3.9 %stats.5 = (f32[4,2,256]{2,1,0:T(2,128)}, f32[4,2,256]{2,1,0:T(2,128)}) custom-call(bf16[256,1024]{1,0:T(8,128)(2,1)} %q_ref.19, bf16[256,1152]{1,0:T(8,128)(2,1)} %copy-done.1, bf16[256,1152]{1,0:T(8,128)(2,1)} %copy-done.1, f32[1,256]{1,0:T(1,128)} %bitcast.15, f32[4,2,256]{2,1,0:T(2,128)} %broadcast_in_dim.32.m_ref, f32[4,2,256]{2,1,0:T(2,128)} %broadcast_in_dim.33.l_ref), custom_call_target="tpu_custom_call" | custom-call | flops 268435456 | bytes 1048576 | tf_op jit(solution)/shard_map/stats/pallas_call | solution.py:133
  36.4 3.9 %stats.6 = (f32[4,2,256]{2,1,0:T(2,128)}, f32[4,2,256]{2,1,0:T(2,128)}) custom-call(bf16[256,1024]{1,0:T(8,128)(2,1)} %q_ref.19, bf16[256,1152]{1,0:T(8,128)(2,1)} %copy-done.3, bf16[256,1152]{1,0:T(8,128)(2,1)} %copy-done.3, f32[1,256]{1,0:T(1,128)} %bitcast.16, f32[4,2,256]{2,1,0:T(2,128)} %get-tuple-element.22.m_ref, f32[4,2,256]{2,1,0:T(2,128)} %get-tuple-element.23.l_ref), custom_call_target="tpu_custom_call" | custom-call | flops 268435456 | bytes 1048576 | tf_op jit(solution)/shard_map/stats/pallas_call | solution.py:133
  40.3 3.9 %stats.7 = (f32[4,2,256]{2,1,0:T(2,128)}, f32[4,2,256]{2,1,0:T(2,128)}) custom-call(bf16[256,1024]{1,0:T(8,128)(2,1)} %q_ref.19, bf16[256,1152]{1,0:T(8,128)(2,1)} %collective-permute-done.3.k_ref.kd_ref.v_ref, bf16[256,1152]{1,0:T(8,128)(2,1)} %collective-permute-done.3.k_ref.kd_ref.v_ref, f32[1,256]{1,0:T(1,128)} %bitcast.17, ...), custom_call_target="tpu_custom_call" | custom-call | flops 268435456 | bytes 1048576 | tf_op jit(solution)/shard_map/stats/pallas_call | solution.py:133
  44.2 3.3 %collective-permute-done.2.k_ref.kd_ref.v_ref = bf16[256,1152]{1,0:T(8,128)(2,1)} collective-permute-done((bf16[256,1152]{1,0:T(8,128)(2,1)S(1)}, bf16[256,1152]{1,0:T(8,128)(2,1)}, u32[]{:S(2)}, u32[]{:S(2)}) %collective-permute-start.2) | collective-permute-done | bytes 589856 | tf_op jit(solution)/shard_map/ppermute | solution.py:84
  47.6 3.9 %stats.8 = (f32[4,2,256]{2,1,0:T(2,128)}, f32[4,2,256]{2,1,0:T(2,128)}) custom-call(bf16[256,1024]{1,0:T(8,128)(2,1)} %q_ref.19, bf16[256,1152]{1,0:T(8,128)(2,1)} %collective-permute-done.2.k_ref.kd_ref.v_ref, bf16[256,1152]{1,0:T(8,128)(2,1)} %collective-permute-done.2.k_ref.kd_ref.v_ref, f32[1,256]{1,0:T(1,128)} %bitcast.18, ...), custom_call_target="tpu_custom_call" | custom-call | flops 268435456 | bytes 1048576 | tf_op jit(solution)/shard_map/stats/pallas_call | solution.py:133
  52.4 3.9 %stats.9.t_ref = f32[4,2,256]{2,1,0:T(2,128)} custom-call(bf16[256,1024]{1,0:T(8,128)(2,1)} %q_ref.19, bf16[256,1152]{1,0:T(8,128)(2,1)} %copy-done.2, bf16[256,1152]{1,0:T(8,128)(2,1)} %copy-done.2, f32[1,256]{1,0:T(1,128)} %bitcast.19, f32[4,2,256]{2,1,0:T(2,128)} %get-tuple-element.28.m_ref, f32[4,2,256]{2,1,0:T(2,128)} %get-tuple-element.29.l_ref), custom_call_target="tpu_custom_call" | custom-call | flops 268435456 | bytes 1048576 | tf_op jit(solution)/shard_map/stats/pallas_call | solution.py:133
  56.2 21.7 %all-gather.2.cloned.1.call-done = bf16[1024,2048]{1,0:T(8,128)(2,1)} async-done(((bf16[1024,128]{1,0:T(8,128)(2,1)}), bf16[1024,2048]{1,0:T(8,128)(2,1)}) %all-gather.2.cloned.1.call-update) | async-done | bytes 4194320 | tf_op jit(solution)/shard_map/all_gather | solution.py:98
  77.9 4.4 %convert_multiply_fusion = (f32[256,1024]{1,0:T(8,128)S(1)}, bf16[256,1024]{1,0:T(8,128)(2,1)}) fusion(bf16[256,1024]{1,0:T(8,128)(2,1)S(1)} %copy-done.8, bf16[256,2048]{1,0:T(8,128)(2,1)S(1)} %copy-done, bf16[1024,2048]{1,0:T(8,128)(2,1)} %all-gather.2.cloned.1.call-done, f32[1024]{0:T(1024)S(1)} %fusion.4), kind=kOutput, calls=%fused_computation.7 | convolution fusion | flops 1081081856 | bytes 7344128 | tf_op jit(solution)/shard_map/dot_general | solution.py:16
  83.2 1.6 reduce_sum.9
  85.6 4.9 %grads.5 = (f32[256,1024]{1,0:T(8,128)}, bf16[2,256,512]{2,1,0:T(8,128)(2,1)}) custom-call(bf16[256,1024]{1,0:T(8,128)(2,1)} %q_ref.19, bf16[256,1024]{1,0:T(8,128)(2,1)} %get-tuple-element.45.a_ref, bf16[256,1152]{1,0:T(8,128)(2,1)} %copy-done.2, bf16[256,1152]{1,0:T(8,128)(2,1)} %copy-done.2, bf16[256,1152]{1,0:T(8,128)(2,1)} %copy-done.2, ...), custom_call_target="tpu_custom_call" | custom-call | flops 1342177280 | bytes 4194304 | tf_op jit(solution)/shard_map/grads/pallas_call | solution.py:164
  90.5 5.2 %grads.6 = (f32[256,1024]{1,0:T(8,128)}, bf16[2,256,512]{2,1,0:T(8,128)(2,1)}) custom-call(bf16[256,1024]{1,0:T(8,128)(2,1)} %q_ref.19, bf16[256,1024]{1,0:T(8,128)(2,1)} %get-tuple-element.45.a_ref, bf16[256,1152]{1,0:T(8,128)(2,1)} %collective-permute-done.2.k_ref.kd_ref.v_ref, bf16[256,1152]{1,0:T(8,128)(2,1)} %collective-permute-done.2.k_ref.kd_ref.v_ref, ...), custom_call_target="tpu_custom_call" | custom-call | flops 1342177280 | bytes 4194304 | tf_op jit(solution)/shard_map/grads/pallas_call | solution.py:164
  95.7 5.3 %grads.7 = (f32[256,1024]{1,0:T(8,128)}, bf16[2,256,512]{2,1,0:T(8,128)(2,1)}) custom-call(bf16[256,1024]{1,0:T(8,128)(2,1)} %q_ref.19, bf16[256,1024]{1,0:T(8,128)(2,1)} %get-tuple-element.45.a_ref, bf16[256,1152]{1,0:T(8,128)(2,1)} %collective-permute-done.3.k_ref.kd_ref.v_ref, bf16[256,1152]{1,0:T(8,128)(2,1)} %collective-permute-done.3.k_ref.kd_ref.v_ref, ...), custom_call_target="tpu_custom_call" | custom-call | flops 1342177280 | bytes 4194304 | tf_op jit(solution)/shard_map/grads/pallas_call | solution.py:164
  101.0 5.2 %grads.8 = (f32[256,1024]{1,0:T(8,128)}, bf16[2,256,512]{2,1,0:T(8,128)(2,1)}) custom-call(bf16[256,1024]{1,0:T(8,128)(2,1)} %q_ref.19, bf16[256,1024]{1,0:T(8,128)(2,1)} %get-tuple-element.45.a_ref, bf16[256,1152]{1,0:T(8,128)(2,1)} %copy-done.3, bf16[256,1152]{1,0:T(8,128)(2,1)} %copy-done.3, bf16[256,1152]{1,0:T(8,128)(2,1)} %copy-done.3, ...), custom_call_target="tpu_custom_call" | custom-call | flops 1342177280 | bytes 4194304 | tf_op jit(solution)/shard_map/grads/pallas_call | solution.py:164
  107.6 1.3 collective-permute-start.7
  111.5 66.1 %reduce-scatter.2.cloned.1.call-done = bf16[128,1024]{1,0:T(8,128)(2,1)} async-done(((bf16[2048,1024]{1,0:T(8,128)(2,1)}), bf16[128,1024]{1,0:T(8,128)(2,1)}) %reduce-scatter.2.cloned.1.call-update) | async-done | bytes 262160 | tf_op jit(solution)/shard_map/reduce_scatter | solution.py:120
  177.6 1.8 convert_element_type.60
  179.4 5.1 %grads.9 = (bf16[256,1024]{1,0:T(8,128)(2,1)}, f32[2,256,512]{2,1,0:T(8,128)}) custom-call(bf16[256,1024]{1,0:T(8,128)(2,1)} %q_ref.19, bf16[256,1024]{1,0:T(8,128)(2,1)} %get-tuple-element.45.a_ref, bf16[256,1152]{1,0:T(8,128)(2,1)} %copy-done.1, bf16[256,1152]{1,0:T(8,128)(2,1)} %copy-done.1, bf16[256,1152]{1,0:T(8,128)(2,1)} %copy-done.1, ...), custom_call_target="tpu_custom_call" | custom-call | flops 1342177280 | bytes 4194304 | tf_op jit(solution)/shard_map/grads/pallas_call | solution.py:164
  185.7 1.6 add_convert_fusion
  (46 shorter events, 13.1 us)
Async XLA Ops:
  7.2 1.2 copy-start
  7.2 70.8 %all-gather.2.cloned.1.call-start = ((), (), s32[]{:S(2)}) async-start(), calls=%async_computation.1 | async-start | bytes 4456448 | tf_op jit(solution)/shard_map/all_gather | solution.py:98
  7.9 169.7 %reduce-scatter.2.cloned.1.call-start = ((), (), s32[]{:S(2)}) async-start(), calls=%async_computation.2 | async-start | bytes 4456448 | tf_op jit(solution)/shard_map/reduce_scatter | solution.py:120
  12.7 0.7 copy-start.7
  12.7 1.3 copy-start.4
  12.7 1.3 copy-start.5
  12.7 16.2 %copy-start.9 = (s32[16]{0:T(128)S(1)}, s32[16]{0:T(128)}, u32[]{:S(2)}) copy-start(s32[16]{0:T(128)} %param.17) | copy-start | bytes 196
  12.7 16.2 %copy-start.6 = (f32[1,16,128]{2,1,0:T(8,128)S(1)}, f32[1,16,128]{2,1,0:T(8,128)}, u32[]{:S(2)}) copy-start(f32[1,16,128]{2,1,0:T(8,128)} %param.16) | copy-start | bytes 24580
  14.1 17.6 %copy-start.1 = (bf16[256,1152]{1,0:T(8,128)(2,1)}, bf16[256,1152]{1,0:T(8,128)(2,1)S(1)}, u32[]{:S(2)}) copy-start(bf16[256,1152]{1,0:T(8,128)(2,1)S(1)} %pad_maximum_fusion.k_ref.kd_ref.v_ref) | copy-start | bytes 1769476
  14.1 21.5 %collective-permute-start.4 = (bf16[256,1152]{1,0:T(8,128)(2,1)S(1)}, bf16[256,1152]{1,0:T(8,128)(2,1)S(1)}, u32[]{:S(2)}, u32[]{:S(2)}) collective-permute-start(bf16[256,1152]{1,0:T(8,128)(2,1)S(1)} %pad_maximum_fusion.k_ref.kd_ref.v_ref), channel_id=1, source_target_pairs={{0,2},{2,4},{4,6},{6,8},{8,10},{10,12},{12,14},{14,16},{16,18},{18... | collective-permute-start | bytes 1769480 | tf_op jit(solution)/shard_map/ppermute | solution.py:84
  16.5 23.8 %collective-permute-start.3 = (bf16[256,1152]{1,0:T(8,128)(2,1)S(1)}, bf16[256,1152]{1,0:T(8,128)(2,1)}, u32[]{:S(2)}, u32[]{:S(2)}) collective-permute-start(bf16[256,1152]{1,0:T(8,128)(2,1)S(1)} %pad_maximum_fusion.k_ref.kd_ref.v_ref), channel_id=1, source_target_pairs={{0,4},{2,6},{4,8},{6,10},{8,12},{10,14},{12,16},{14,18},{16,20},{1... | collective-permute-start | bytes 1769480 | tf_op jit(solution)/shard_map/ppermute | solution.py:84
  21.8 25.8 %collective-permute-start.2 = (bf16[256,1152]{1,0:T(8,128)(2,1)S(1)}, bf16[256,1152]{1,0:T(8,128)(2,1)}, u32[]{:S(2)}, u32[]{:S(2)}) collective-permute-start(bf16[256,1152]{1,0:T(8,128)(2,1)S(1)} %pad_maximum_fusion.k_ref.kd_ref.v_ref), channel_id=1, source_target_pairs={{0,6},{2,8},{4,10},{6,12},{8,14},{10,16},{12,18},{14,20},{16,22},{... | collective-permute-start | bytes 1769480 | tf_op jit(solution)/shard_map/ppermute | solution.py:84
  26.1 25.4 %collective-permute-start.1 = (bf16[256,1152]{1,0:T(8,128)(2,1)S(1)}, bf16[256,1152]{1,0:T(8,128)(2,1)S(1)}, u32[]{:S(2)}, u32[]{:S(2)}) collective-permute-start(bf16[256,1152]{1,0:T(8,128)(2,1)S(1)} %pad_maximum_fusion.k_ref.kd_ref.v_ref), channel_id=1, source_target_pairs={{0,8},{2,10},{4,12},{6,14},{8,16},{10,18},{12,20},{14,22},{16,24},... | collective-permute-start | bytes 1769480 | tf_op jit(solution)/shard_map/ppermute | solution.py:84
  29.0 6.6 %collective-permute-start = (f32[16,128]{1,0:T(8,128)S(1)}, f32[16,128]{1,0:T(8,128)S(1)}, u32[]{:S(2)}, u32[]{:S(2)}) collective-permute-start(f32[16,128]{1,0:T(8,128)S(1)} %bitcast_select_fusion), channel_id=1, source_target_pairs={{0,1},{1,0},{2,3},{3,2},{4,5},{5,4},{6,7},{7,6},{8,9},{9,8},{10,11... | collective-permute-start | bytes 24584 | tf_op jit(solution)/shard_map/ppermute | solution.py:110
  31.7 46.3 %copy-start.8 = (bf16[256,1024]{1,0:T(8,128)(2,1)S(1)}, bf16[256,1024]{1,0:T(8,128)(2,1)}, u32[]{:S(2)}) copy-start(bf16[256,1024]{1,0:T(8,128)(2,1)} %param.12) | copy-start | bytes 1572868
  35.6 0.8 copy-start.3
  51.5 0.8 copy-start.2
  106.3 78.2 %collective-permute-start.8 = (bf16[2,256,512]{2,1,0:T(8,128)(2,1)}, bf16[2,256,512]{2,1,0:T(8,128)(2,1)S(1)}, u32[]{:S(2)}, u32[]{:S(2)}) collective-permute-start(bf16[2,256,512]{2,1,0:T(8,128)(2,1)} %get-tuple-element.38), channel_id=1, source_target_pairs={{2,0},{4,2},{6,4},{8,6},{10,8},{12,10},{14,12},{16,14},{18,16},{20... | collective-permute-start | bytes 1572872 | tf_op jit(solution)/shard_map/ppermute | solution.py:84
  107.6 77.0 %collective-permute-start.7 = (bf16[2,256,512]{2,1,0:T(8,128)(2,1)}, bf16[2,256,512]{2,1,0:T(8,128)(2,1)S(1)}, u32[]{:S(2)}, u32[]{:S(2)}) collective-permute-start(bf16[2,256,512]{2,1,0:T(8,128)(2,1)} %get-tuple-element.37), channel_id=1, source_target_pairs={{4,0},{6,2},{8,4},{10,6},{12,8},{14,10},{16,12},{18,14},{20,16},{2... | collective-permute-start | bytes 1572872 | tf_op jit(solution)/shard_map/ppermute | solution.py:84
  108.9 75.7 %collective-permute-start.6 = (bf16[2,256,512]{2,1,0:T(8,128)(2,1)}, bf16[2,256,512]{2,1,0:T(8,128)(2,1)S(1)}, u32[]{:S(2)}, u32[]{:S(2)}) collective-permute-start(bf16[2,256,512]{2,1,0:T(8,128)(2,1)} %get-tuple-element.36), channel_id=1, source_target_pairs={{6,0},{8,2},{10,4},{12,6},{14,8},{16,10},{18,12},{20,14},{22,16},{... | collective-permute-start | bytes 1572872 | tf_op jit(solution)/shard_map/ppermute | solution.py:84
  110.2 75.6 %collective-permute-start.5 = (bf16[2,256,512]{2,1,0:T(8,128)(2,1)}, bf16[2,256,512]{2,1,0:T(8,128)(2,1)S(1)}, u32[]{:S(2)}, u32[]{:S(2)}) collective-permute-start(bf16[2,256,512]{2,1,0:T(8,128)(2,1)} %get-tuple-element.35), channel_id=1, source_target_pairs={{8,0},{10,2},{12,4},{14,6},{16,8},{18,10},{20,12},{22,14},{24,16},... | collective-permute-start | bytes 1572872 | tf_op jit(solution)/shard_map/ppermute | solution.py:84
Sparse Core Ops, SparseCore 0:
  10.1 67.7 all-gather.1
  81.8 95.7 reduce-scatter.1

commit v2 on v1

--- a/solution.py
+++ b/solution.py
@@ -3,6 +3,7 @@
 import jax.numpy as jnp
 from jax import lax
 from jax.experimental import pallas as pl
+from jax.experimental.pallas import tpu as pltpu
 from jax.sharding import PartitionSpec as P
 
 HEAD_WIDTH = 128
@@ -79,6 +80,107 @@
         dq_ref[:, cols] = part.astype(dq_ref.dtype)
 
 
+def gather_orders(count):
+    bits = count.bit_length() - 1
+    top, middle = [bits - 1, bits - 2], list(range(bits - 3, 0, -1))
+    return (top + middle + [0], middle + top + [0])
+
+
+def gather_kernel(count, code_ref, out_ref, send_sem, recv_sem):
+    me = lax.axis_index("ctx")
+    bits = count.bit_length() - 1
+    half = code_ref.shape[0] // 2
+    step = [(1 - 2 * ((me // (1 << b)) % 2)) * (1 << b) for b in range(bits)]
+
+    def moved(mask):
+        return me + sum(step[b] for b in range(bits) if mask >> b & 1)
+
+    barrier = pltpu.get_barrier_semaphore()
+    for b in range(bits):
+        pl.semaphore_signal(
+            barrier,
+            inc=1,
+            device_id={"ctx": moved(1 << b)},
+            device_id_type=pl.DeviceIdType.MESH,
+        )
+    pl.semaphore_wait(barrier, bits)
+
+    def transfer(part, mask, bit):
+        rows = pl.ds(part * half, half)
+        source = code_ref.at[rows] if mask == 0 else out_ref.at[moved(mask), rows]
+        slot = part * count + (mask | 1 << bit)
+        return pltpu.make_async_remote_copy(
+            src_ref=source,
+            dst_ref=out_ref.at[moved(mask), rows],
+            send_sem=send_sem.at[slot],
+            recv_sem=recv_sem.at[slot],
+            device_id={"ctx": moved(1 << bit)},
+            device_id_type=pl.DeviceIdType.MESH,
+        )
+
+    orders = gather_orders(count)
+    held = [[0], [0]]
+    started = []
+    arrived = [{}, {}]
+    for stage in range(bits):
+        for part in range(2):
+            bit = orders[part][stage]
+            new = []
+            for mask in held[part]:
+                if mask in arrived[part]:
+                    arrived[part].pop(mask).wait_recv()
+                copy = transfer(part, mask, bit)
+                copy.start()
+                started.append(copy)
+                new.append(mask | 1 << bit)
+                arrived[part][mask | 1 << bit] = copy
+            held[part] = held[part] + new
+        if stage == 0:
+            out_ref[me] = code_ref[...]
+    for part in range(2):
+        for copy in arrived[part].values():
+            copy.wait_recv()
+    for copy in started:
+        copy.wait_send()
+
+
+def gather(codes, count):
+    return pl.pallas_call(
+        functools.partial(gather_kernel, count),
+        out_shape=jax.ShapeDtypeStruct((count, *codes.shape), codes.dtype),
+        in_specs=[pl.BlockSpec(memory_space=pltpu.VMEM)],
+        out_specs=pl.BlockSpec(memory_space=pltpu.VMEM),
+        scratch_shapes=[pltpu.SemaphoreType.DMA((2 * count,))] * 2,
+        compiler_params=pltpu.CompilerParams(collective_id=0, has_side_effects=True),
+        cost_estimate=pl.CostEstimate(flops=0, bytes_accessed=100 << 20, transcendentals=0),
+        name="gather",
+    )(codes)
+
+
+def project_kernel(pairs, y_ref, code_ref, scale_ref, o_ref, a_ref, d_ref):
+    scales = scale_ref[...]
+    weight = jnp.concatenate(
+        [
+            (code_ref[c].astype(jnp.float32) * scales).astype(jnp.bfloat16)
+            for c in range(code_ref.shape[0])
+        ],
+        axis=1,
+    )
+    grads = dot(y_ref[...], weight, LAST).astype(jnp.bfloat16)
+    a_ref[...] = grads
+    product = grads.astype(jnp.float32) * o_ref[...].astype(jnp.float32)
+    for j in range(pairs):
+        cols = slice(j * HEAD_WIDTH, (j + 1) * HEAD_WIDTH)
+        d_ref[0, j : j + 1, :] = jnp.sum(product[:, cols].T, axis=0, keepdims=True)
+
+
+def plane_turn(x, plane, by):
+    size = lax.axis_size("ctx")
+    return lax.ppermute(
+        x, "ctx", [(i, i // plane * plane + (i % plane + by) % plane) for i in range(size)]
+    )
+
+
 def shift_by(x, axis, by):
     size = lax.axis_size(axis)
     return lax.ppermute(x, axis, [(i, i + by) for i in range(size) if 0 <= i + by < size])
@@ -95,14 +197,23 @@
     steps = ctx_count // 4 + 1
     scale = HEAD_WIDTH ** (-0.5)
 
-    gathered = lax.all_gather(codes, "ctx", axis=1, tiled=True)
+    ctx_index = lax.axis_index("ctx")
+    plane = steps - 1
+    place = ctx_index % plane
+    bits = ctx_count.bit_length() - 1
+
+    gathered = gather(codes, ctx_count)
 
     docs = (doc_ids + 1).astype(jnp.bfloat16)
     packed = jnp.concatenate(
         [key, value, jnp.broadcast_to(docs[:, None], (rows, HEAD_WIDTH))], axis=1
     )
     query_docs = (doc_ids + 1).astype(jnp.float32)[None, :]
-    blocks = [packed] + [shift_by(packed, "ctx", d) for d in range(1, steps)]
+    before = shift_by(packed, "ctx", plane)
+    blocks = [packed]
+    for d in range(1, plane):
+        blocks.append(plane_turn(jnp.where(place + d < plane, packed, before), plane, d))
+    blocks.append(before)
 
     masked_table = jnp.where((holder == shard_index)[:, None], scale_copies[0], 0.0)
     scale_table = masked_table
@@ -114,10 +225,21 @@
         heads * HEAD_WIDTH
     )
 
-    partial_weight = (
-        dot(grad_y, attention_output, FIRST) * (rows * ctx_count) ** (-0.5)
-    ).astype(jnp.bfloat16)
-    scattered = lax.psum_scatter(partial_weight, "ctx", scatter_dimension=0, tiled=True)
+    columns = attention_output.shape[1]
+    summed_weight = dot(grad_y, attention_output, FIRST) * (rows * ctx_count) ** (-0.5)
+    summed_weight = summed_weight.reshape(ctx_count, -1, columns)
+    left = list(range(bits))
+    for bit in [0] + list(range(1, bits)):
+        shape = summed_weight.shape
+        low = 1 << left.index(bit)
+        left.remove(bit)
+        split = summed_weight.reshape(shape[0] // (2 * low), 2, low, *shape[1:])
+        mine = (ctx_index // (1 << bit)) % 2
+        kept = lax.dynamic_index_in_dim(split, mine, 1, keepdims=False)
+        sent = lax.dynamic_index_in_dim(split, 1 - mine, 1, keepdims=False).astype(jnp.bfloat16)
+        got = lax.ppermute(sent, "ctx", [(i, i ^ (1 << bit)) for i in range(ctx_count)])
+        summed_weight = (kept + got.astype(jnp.float32)).reshape(shape[0] // 2, *shape[1:])
+    grad_weight = summed_weight[0]
 
     pair_spec = pl.BlockSpec((rows, pairs * HEAD_WIDTH), lambda g: (0, g))
     key_spec = pl.BlockSpec((rows, HEAD_WIDTH), lambda g: (0, g))
@@ -147,13 +269,34 @@
         state = stats(blocks[d], state, d == 0, d == steps - 1)
     log_total = state[0]
 
-    weight = (gathered.astype(jnp.float32) * row_scale[:, None]).astype(jnp.bfloat16)
-    attention_gradient = dot(grad_y, weight, LAST).astype(jnp.bfloat16)
-    row_delta = jnp.sum(
-        attention_gradient.reshape(rows, groups, pairs, HEAD_WIDTH).astype(jnp.float32)
-        * attention_output.reshape(rows, groups, pairs, HEAD_WIDTH).astype(jnp.float32),
-        axis=-1,
-    ).transpose(1, 2, 0)
+    if codes.shape[1] % HEAD_WIDTH == 0:
+        attention_gradient, row_delta = pl.pallas_call(
+            functools.partial(project_kernel, pairs),
+            grid=(groups,),
+            in_specs=[
+                pl.BlockSpec(grad_y.shape, lambda g: (0, 0)),
+                pl.BlockSpec((ctx_count, pairs * HEAD_WIDTH, codes.shape[1]), lambda g: (0, g, 0)),
+                pl.BlockSpec((pairs * HEAD_WIDTH, 1), lambda g: (g, 0)),
+                pair_spec,
+            ],
+            out_specs=[pair_spec, row_spec],
+            out_shape=[jax.ShapeDtypeStruct(query.shape, jnp.bfloat16), row_shape],
+            cost_estimate=pl.CostEstimate(
+                flops=2 * rows * grad_y.shape[1] * query.shape[1],
+                bytes_accessed=6 << 20,
+                transcendentals=0,
+            ),
+            name="project",
+        )(grad_y, gathered, row_scale[:, None], attention_output)
+    else:
+        weight = (gathered.astype(jnp.float32) * row_scale[None, :, None]).astype(jnp.bfloat16)
+        weight = weight.transpose(1, 0, 2).reshape(codes.shape[0], -1)
+        attention_gradient = dot(grad_y, weight, LAST).astype(jnp.bfloat16)
+        row_delta = jnp.sum(
+            attention_gradient.reshape(rows, groups, pairs, HEAD_WIDTH).astype(jnp.float32)
+            * attention_output.reshape(rows, groups, pairs, HEAD_WIDTH).astype(jnp.float32),
+            axis=-1,
+        ).transpose(1, 2, 0)
 
     def grads(block, total, own):
         first = total is None
@@ -187,16 +330,30 @@
         )
 
     total = None
-    parts = []
-    for d in reversed(range(steps)):
+    turned = {}
+    for d in grads_order(plane):
         total, part = grads(blocks[d], total, d == 0)
-        if d:
-            part = shift_by(part, "ctx", -d)
-        parts.append(part)
-    summed = sum(part.astype(jnp.float32) for part in parts).astype(jnp.bfloat16)
+        if d == plane:
+            far = part
+        elif d == 0:
+            near = part
+        else:
+            turned[d] = plane_turn(part, plane, -d)
+    wrapped = far.astype(jnp.float32)
+    for d in range(1, plane):
+        wrapped = wrapped + jnp.where(place + d >= plane, turned[d].astype(jnp.float32), 0.0)
+    wrapped = shift_by(wrapped.astype(jnp.bfloat16), "ctx", -plane)
+    for d in range(1, plane):
+        near = near + jnp.where(place + d < plane, turned[d].astype(jnp.float32), 0.0)
+    summed = (near + wrapped.astype(jnp.float32)).astype(jnp.bfloat16)
     key_gradient, value_gradient = summed[0], summed[1]
-    grad_weight = scattered.astype(jnp.float32)
     return (total, key_gradient, value_gradient, grad_weight)
+
+
+def grads_order(plane):
+    inner = list(range(1, plane))
+    inner.sort(key=lambda d: abs(2 * d - plane))
+    return inner + [plane, 0]
 
 
 def solution(mesh):

time: 196 us -> 199 us (1.015)
  Pallas kernels: 45.4 us -> 108 us
  waiting for transfers between devices: 93.1 us -> 40.2 us
  between operations: 14.3 us -> 1.01 us
  other arithmetic: 5.6 us -> 14 us
  local copies, waits for them, and re-layouts: 6.53 us -> 14.6 us
  matrix products: 8.66 us -> 2.64 us
  starting transfers between devices: 21.5 us -> 17.9 us
    reduce_scatter x1 -> x0, waiting for transfers between devices: 66.1 us -> none  [per_device(): lax.psum_scatter(partial_weight, 'ctx', scatter_dimension=0, tiled=True)]
    pallas_call x0 -> x2, Pallas kernels: none -> 63.1 us  [the longest x1 57.5 us: gather(): pl.pallas_call(functools.partial(gather_kernel, count), out_shape=jax.Sha...]
    ppermute x0 -> x10, waiting for transfers between devices: none -> 23 us  [the longest x6 14.2 us: plane_turn(): lax.ppermute(x, 'ctx', [(i, i // plane * plane + (i % plane + by) % plane...]
    all_gather x1 -> x0, waiting for transfers between devices: 21.7 us -> none  [per_device(): gathered = lax.all_gather(codes, 'ctx', axis=1, tiled=True)]
    ppermute x8 -> x2, starting transfers between devices: 19.9 us -> 5.78 us  [shift_by(): lax.ppermute(x, axis, [(i, i + by) for i in range(size) if 0 <= i + by <...]
    ppermute x8 -> x2, waiting for transfers between devices: 4.54 us -> 17.2 us  [shift_by(): lax.ppermute(x, axis, [(i, i + by) for i in range(size) if 0 <= i + by <...]
    ppermute x0 -> x10, starting transfers between devices: none -> 10.6 us  [the longest x6 6.31 us: plane_turn(): lax.ppermute(x, 'ctx', [(i, i // plane * plane + (i % plane + by) % plane...]
    add x0 -> x4, other arithmetic: none -> 6.99 us  [the longest x3 6.98 us: per_device(): kept + got.astype(jnp.float32)]
  transfers between devices with their start and end apart: 11 -> 13, of which waited for: 4 -> 6; matrix products, arithmetic and copies ran while one was open for 8% -> 9% of each run, Pallas kernels for 23% -> 54%
where the time goes in v2:
time: 199 us; the launch traced here: 198 us
  Pallas kernels  108 us (54%)
  waiting for transfers between devices  40.2 us (20%)
  starting transfers between devices  17.9 us (9%)
  local copies, waits for them, and re-layouts  14.6 us (7%)
  other arithmetic  14 us (7%)
  matrix products  2.64 us (1%)
    pallas_call x1, Pallas kernels, gather(): pl.pallas_call(functools.partial(gather_kernel, count), out_shape=jax.Sha...  57.5 us
    pallas_call x5, Pallas kernels, grads(): pl.pallas_call(functools.partial(grads_kernel, own, first, pairs, scale),...  25.5 us
    pallas_call x5, Pallas kernels, stats(): pl.pallas_call(functools.partial(stats_kernel, own, final, pairs, scale),...  19.4 us
    ppermute x2, waiting for transfers between devices, shift_by(): lax.ppermute(x, axis, [(i, i + by) for i in range(size) if 0 <= i + by <...  17.2 us
    ppermute x6, waiting for transfers between devices, plane_turn(): lax.ppermute(x, 'ctx', [(i, i // plane * plane + (i % plane + by) % plane...  14.2 us
    ppermute x4, waiting for transfers between devices, per_device(): lax.ppermute(sent, 'ctx', [(i, i ^ 1 << bit) for i in range(ctx_count)])  8.76 us
    unnamed x26, local copies, waits for them, and re-layouts  7.72 us
    add x3, other arithmetic, per_device(): kept + got.astype(jnp.float32)  6.98 us
  transfers between devices with their start and end apart: 13, of which 6 were waited for; matrix products, arithmetic and copies ran while one was open for 9% of the time, Pallas kernels for 54%

profile of v2, /device:TPU:0, one launch (start us, length us, event | category | flops | bytes accessed | tf_op | source)
XLA Modules:
  0.0 198.4 jit_solution(10223837806869893159)
XLA Ops:
  0.6 2.6 %convolution_multiply_fusion = f32[2048,1024]{1,0:T(8,128)S(1)} fusion(bf16[256,2048]{1,0:T(8,128)(2,1)} %y_ref.1, bf16[256,1024]{1,0:T(8,128)(2,1)} %o_ref.1), kind=kOutput, calls=%fused_computation | convolution fusion | flops 1075838976 | bytes 9961472 | tf_op jit(solution)/shard_map/dot_general | solution.py:17
  3.3 3.3 %copy-done = f32[2048,1024]{1,0:T(8,128)} copy-done((f32[2048,1024]{1,0:T(8,128)}, f32[2048,1024]{1,0:T(8,128)S(1)}, u32[]{:S(2)}) %copy-start) | copy-done | bytes 8388632
  9.5 4.5 %collective-permute-start.1 = (bf16[256,1152]{1,0:T(8,128)(2,1)S(1)}, bf16[256,1152]{1,0:T(8,128)(2,1)S(1)}, u32[]{:S(2)}, u32[]{:S(2)}) collective-permute-start(bf16[256,1152]{1,0:T(8,128)(2,1)S(1)} %pad_maximum_fusion.k_ref.kd_ref.v_ref), channel_id=1, source_target_pairs={{0,8},{2,10},{4,12},{6,14},{8,16},{10,18},{12,20},{14,22},{16,24},... | collective-permute-start | bytes 1769480 | tf_op jit(solution)/shard_map/ppermute | solution.py:186
  14.0 13.1 %collective-permute-done.1.k_ref.kd_ref.v_ref = bf16[256,1152]{1,0:T(8,128)(2,1)S(1)} collective-permute-done((bf16[256,1152]{1,0:T(8,128)(2,1)S(1)}, bf16[256,1152]{1,0:T(8,128)(2,1)S(1)}, u32[]{:S(2)}, u32[]{:S(2)}) %collective-permute-start.1) | collective-permute-done | bytes 589856 | tf_op jit(solution)/shard_map/ppermute | solution.py:186
  31.7 3.5 %bitcast_add_fusion = f32[8,1,128,1024]{3,2,0,1:T(8,128)S(1)} fusion(bf16[8,1,128,1024]{3,2,0,1:T(8,128)(2,1)} %collective-permute-done.9, f32[8,2,1,128,1024]{4,3,1,0,2:T(8,128)} %bitcast.32, s32[]{:T(128)S(6)} %select_n.149), kind=kLoop, calls=%fused_computation.2 | loop fusion | flops 2097152 | bytes 10485764 | tf_op jit(solution)/shard_map/add | solution.py:241
  35.2 1.9 copy-done.1
  41.6 3.8 %stats.5 = (f32[4,2,256]{2,1,0:T(2,128)}, f32[4,2,256]{2,1,0:T(2,128)}) custom-call(bf16[256,1024]{1,0:T(8,128)(2,1)} %q_ref.19, bf16[256,1152]{1,0:T(8,128)(2,1)} %copy-done.3, bf16[256,1152]{1,0:T(8,128)(2,1)} %copy-done.3, f32[1,256]{1,0:T(1,128)} %bitcast.37, f32[4,2,256]{2,1,0:T(2,128)} %broadcast_in_dim.41.m_ref, f32[4,2,256]{2,1,0:T(2,128)} %broadcast_in_dim.42.l_ref), custom_call_target="tpu_custom_call" | custom-call | flops 268435456 | bytes 1048576 | tf_op jit(solution)/shard_map/stats/pallas_call | solution.py:255
  45.4 57.5 %gather.1.code_ref = bf16[16,1024,128]{2,1,0:T(8,128)(2,1)} custom-call(bf16[1024,128]{1,0:T(8,128)(2,1)} %code_ref.1), custom_call_target="tpu_custom_call" | custom-call | bytes 104857600 | tf_op jit(solution)/shard_map/gather/pallas_call | solution.py:148
  104.0 5.6 %project.1 = (bf16[256,1024]{1,0:T(8,128)(2,1)}, f32[4,2,256]{2,1,0:T(2,128)}) custom-call(bf16[256,2048]{1,0:T(8,128)(2,1)} %y_ref.1, bf16[16,1024,128]{2,1,0:T(8,128)(2,1)} %gather.1.code_ref, f32[1024,1]{1,0:T(8,128)} %copy.14.scale_ref, bf16[256,1024]{1,0:T(8,128)(2,1)} %o_ref.1), custom_call_target="tpu_custom_call" | custom-call | flops 1073741824 | bytes 6291456 | tf_op jit(solution)/shard_map/project/pallas_call | solution.py:273
  110.4 3.9 %stats.6 = (f32[4,2,256]{2,1,0:T(2,128)}, f32[4,2,256]{2,1,0:T(2,128)}) custom-call(bf16[256,1024]{1,0:T(8,128)(2,1)} %q_ref.19, bf16[256,1152]{1,0:T(8,128)(2,1)} %copy-done.4, bf16[256,1152]{1,0:T(8,128)(2,1)} %copy-done.4, f32[1,256]{1,0:T(1,128)} %bitcast.38, f32[4,2,256]{2,1,0:T(2,128)} %get-tuple-element.25.m_ref, f32[4,2,256]{2,1,0:T(2,128)} %get-tuple-element.26.l_ref), custom_call_target="tpu_custom_call" | custom-call | flops 268435456 | bytes 1048576 | tf_op jit(solution)/shard_map/stats/pallas_call | solution.py:255
  115.2 3.9 %stats.7 = (f32[4,2,256]{2,1,0:T(2,128)}, f32[4,2,256]{2,1,0:T(2,128)}) custom-call(bf16[256,1024]{1,0:T(8,128)(2,1)} %q_ref.19, bf16[256,1152]{1,0:T(8,128)(2,1)} %copy-done.6, bf16[256,1152]{1,0:T(8,128)(2,1)} %copy-done.6, f32[1,256]{1,0:T(1,128)} %bitcast.39, f32[4,2,256]{2,1,0:T(2,128)} %get-tuple-element.27.m_ref, f32[4,2,256]{2,1,0:T(2,128)} %get-tuple-element.28.l_ref), custom_call_target="tpu_custom_call" | custom-call | flops 268435456 | bytes 1048576 | tf_op jit(solution)/shard_map/stats/pallas_call | solution.py:255
  119.9 3.9 %stats.8 = (f32[4,2,256]{2,1,0:T(2,128)}, f32[4,2,256]{2,1,0:T(2,128)}) custom-call(bf16[256,1024]{1,0:T(8,128)(2,1)} %q_ref.19, bf16[256,1152]{1,0:T(8,128)(2,1)} %copy-done.5, bf16[256,1152]{1,0:T(8,128)(2,1)} %copy-done.5, f32[1,256]{1,0:T(1,128)} %bitcast.40, f32[4,2,256]{2,1,0:T(2,128)} %get-tuple-element.29.m_ref, f32[4,2,256]{2,1,0:T(2,128)} %get-tuple-element.30.l_ref), custom_call_target="tpu_custom_call" | custom-call | flops 268435456 | bytes 1048576 | tf_op jit(solution)/shard_map/stats/pallas_call | solution.py:255
  123.9 3.9 %stats.9.t_ref = f32[4,2,256]{2,1,0:T(2,128)} custom-call(bf16[256,1024]{1,0:T(8,128)(2,1)} %q_ref.19, bf16[256,1152]{1,0:T(8,128)(2,1)} %copy-done.2, bf16[256,1152]{1,0:T(8,128)(2,1)} %copy-done.2, f32[1,256]{1,0:T(1,128)} %bitcast.41, f32[4,2,256]{2,1,0:T(2,128)} %get-tuple-element.31.m_ref, f32[4,2,256]{2,1,0:T(2,128)} %get-tuple-element.32.l_ref), custom_call_target="tpu_custom_call" | custom-call | flops 268435456 | bytes 1048576 | tf_op jit(solution)/shard_map/stats/pallas_call | solution.py:255
  127.8 4.9 %grads.5 = (f32[256,1024]{1,0:T(8,128)}, bf16[2,256,512]{2,1,0:T(8,128)(2,1)}) custom-call(bf16[256,1024]{1,0:T(8,128)(2,1)} %q_ref.19, bf16[256,1024]{1,0:T(8,128)(2,1)} %get-tuple-element.24.a_ref, bf16[256,1152]{1,0:T(8,128)(2,1)} %copy-done.6, bf16[256,1152]{1,0:T(8,128)(2,1)} %copy-done.6, bf16[256,1152]{1,0:T(8,128)(2,1)} %copy-done.6, ...), custom_call_target="tpu_custom_call" | custom-call | flops 1342177280 | bytes 4194304 | tf_op jit(solution)/shard_map/grads/pallas_call | solution.py:307
  132.7 5.1 %grads.6 = (f32[256,1024]{1,0:T(8,128)}, bf16[2,256,512]{2,1,0:T(8,128)(2,1)}) custom-call(bf16[256,1024]{1,0:T(8,128)(2,1)} %q_ref.19, bf16[256,1024]{1,0:T(8,128)(2,1)} %get-tuple-element.24.a_ref, bf16[256,1152]{1,0:T(8,128)(2,1)} %copy-done.4, bf16[256,1152]{1,0:T(8,128)(2,1)} %copy-done.4, bf16[256,1152]{1,0:T(8,128)(2,1)} %copy-done.4, ...), custom_call_target="tpu_custom_call" | custom-call | flops 1342177280 | bytes 4194304 | tf_op jit(solution)/shard_map/grads/pallas_call | solution.py:307
  137.9 5.1 %grads.7 = (f32[256,1024]{1,0:T(8,128)}, bf16[2,256,512]{2,1,0:T(8,128)(2,1)}) custom-call(bf16[256,1024]{1,0:T(8,128)(2,1)} %q_ref.19, bf16[256,1024]{1,0:T(8,128)(2,1)} %get-tuple-element.24.a_ref, bf16[256,1152]{1,0:T(8,128)(2,1)} %copy-done.5, bf16[256,1152]{1,0:T(8,128)(2,1)} %copy-done.5, bf16[256,1152]{1,0:T(8,128)(2,1)} %copy-done.5, ...), custom_call_target="tpu_custom_call" | custom-call | flops 1342177280 | bytes 4194304 | tf_op jit(solution)/shard_map/grads/pallas_call | solution.py:307
  146.3 2.2 %bitcast_add_fusion.1 = f32[4,1,128,1024]{3,2,0,1:T(8,128)S(1)} fusion(bf16[4,1,128,1024]{3,2,0,1:T(8,128)(2,1)} %collective-permute-done.10, f32[4,2,1,128,1024]{4,3,1,0,2:T(8,128)} %bitcast.34, s32[]{:T(128)S(6)} %select_n.153), kind=kLoop, calls=%fused_computation.4 | loop fusion | flops 1048576 | bytes 5242884 | tf_op jit(solution)/shard_map/add | solution.py:241
  149.4 5.2 %grads.8 = (f32[256,1024]{1,0:T(8,128)}, bf16[2,256,512]{2,1,0:T(8,128)(2,1)}) custom-call(bf16[256,1024]{1,0:T(8,128)(2,1)} %q_ref.19, bf16[256,1024]{1,0:T(8,128)(2,1)} %get-tuple-element.24.a_ref, bf16[256,1152]{1,0:T(8,128)(2,1)} %copy-done.2, bf16[256,1152]{1,0:T(8,128)(2,1)} %copy-done.2, bf16[256,1152]{1,0:T(8,128)(2,1)} %copy-done.2, ...), custom_call_target="tpu_custom_call" | custom-call | flops 1342177280 | bytes 4194304 | tf_op jit(solution)/shard_map/grads/pallas_call | solution.py:307
  157.4 11.4 %collective-permute-done.6 = bf16[2,256,512]{2,1,0:T(8,128)(2,1)} collective-permute-done((bf16[2,256,512]{2,1,0:T(8,128)(2,1)}, bf16[2,256,512]{2,1,0:T(8,128)(2,1)}, u32[]{:S(2)}, u32[]{:S(2)}) %collective-permute-start.6) | collective-permute-done | bytes 524320 | tf_op jit(solution)/shard_map/ppermute | solution.py:179
  168.8 2.4 %fusion.9 = bf16[2,256,512]{2,1,0:T(8,128)(2,1)} fusion(bf16[2,256,512]{2,1,0:T(8,128)(2,1)S(1)} %collective-permute-done.5, bf16[2,256,512]{2,1,0:T(8,128)(2,1)} %collective-permute-done.6, bf16[2,256,512]{2,1,0:T(8,128)(2,1)S(1)} %collective-permute-done.7, bf16[2,256,512]{2,1,0:T(8,128)(2,1)} %get-tuple-element.43, pred[]{:T(512)S(6)} %ge.11, ...), kind=kLoop, calls=%fused_computation.20 | loop fusion | flops 2883584 | bytes 2621443 | tf_op jit(solution)/shard_map/convert_element_type | solution.py:345
  172.5 5.1 %grads.9 = (bf16[256,1024]{1,0:T(8,128)(2,1)}, f32[2,256,512]{2,1,0:T(8,128)}) custom-call(bf16[256,1024]{1,0:T(8,128)(2,1)} %q_ref.19, bf16[256,1024]{1,0:T(8,128)(2,1)} %get-tuple-element.24.a_ref, bf16[256,1152]{1,0:T(8,128)(2,1)} %copy-done.3, bf16[256,1152]{1,0:T(8,128)(2,1)} %copy-done.3, bf16[256,1152]{1,0:T(8,128)(2,1)} %copy-done.3, ...), custom_call_target="tpu_custom_call" | custom-call | flops 1342177280 | bytes 4194304 | tf_op jit(solution)/shard_map/grads/pallas_call | solution.py:307
  178.9 3.3 %collective-permute-start.12 = (bf16[1,1,128,1024]{3,2,0,1:T(8,128)(2,1)S(1)}, bf16[1,1,128,1024]{3,2,0,1:T(8,128)(2,1)S(1)}, u32[]{:S(2)}, u32[]{:S(2)}) collective-permute-start(bf16[1,1,128,1024]{3,2,0,1:T(8,128)(2,1)S(1)} %dynamic-slice_convert_fusion.2), channel_id=1, source_target_pairs={{0,16},{2,18},{4,20},{6,22},{8,24},{10,26},{12,28},{14,30},{16,0},... | collective-permute-start | bytes 786440 | tf_op jit(solution)/shard_map/ppermute | solution.py:240
  182.3 4.1 %collective-permute-done.8 = bf16[2,256,512]{2,1,0:T(8,128)(2,1)} collective-permute-done((bf16[2,256,512]{2,1,0:T(8,128)(2,1)}, bf16[2,256,512]{2,1,0:T(8,128)(2,1)}, u32[]{:S(2)}, u32[]{:S(2)}) %collective-permute-start.8) | collective-permute-done | bytes 524320 | tf_op jit(solution)/shard_map/ppermute | solution.py:186
  188.8 8.8 %collective-permute-done.12 = bf16[1,1,128,1024]{3,2,0,1:T(8,128)(2,1)S(1)} collective-permute-done((bf16[1,1,128,1024]{3,2,0,1:T(8,128)(2,1)S(1)}, bf16[1,1,128,1024]{3,2,0,1:T(8,128)(2,1)S(1)}, u32[]{:S(2)}, u32[]{:S(2)}) %collective-permute-start.12) | collective-permute-done | bytes 262176 | tf_op jit(solution)/shard_map/ppermute | solution.py:240
  (62 shorter events, 28.3 us)
Async XLA Ops:
  3.3 3.3 %copy-start = (f32[2048,1024]{1,0:T(8,128)}, f32[2048,1024]{1,0:T(8,128)S(1)}, u32[]{:S(2)}) copy-start(f32[2048,1024]{1,0:T(8,128)S(1)} %convolution_multiply_fusion) | copy-start | bytes 25165828
  6.6 2.2 %copy-start.11 = (s32[256]{0:T(256)S(1)}, s32[256]{0:T(256)}, u32[]{:S(2)}) copy-start(s32[256]{0:T(256)} %param.14) | copy-start | bytes 3076
  6.6 2.8 %copy-start.8 = (bf16[256,512]{1,0:T(8,128)(2,1)S(1)}, bf16[256,512]{1,0:T(8,128)(2,1)}, u32[]{:S(2)}) copy-start(bf16[256,512]{1,0:T(8,128)(2,1)} %param.11) | copy-start | bytes 786436
  6.6 2.8 %copy-start.9 = (bf16[256,512]{1,0:T(8,128)(2,1)S(1)}, bf16[256,512]{1,0:T(8,128)(2,1)}, u32[]{:S(2)}) copy-start(bf16[256,512]{1,0:T(8,128)(2,1)} %param.10) | copy-start | bytes 786436
  8.3 23.4 %collective-permute-start.9 = (bf16[8,1,128,1024]{3,2,0,1:T(8,128)(2,1)}, bf16[8,1,128,1024]{3,2,0,1:T(8,128)(2,1)}, u32[]{:S(2)}, u32[]{:S(2)}) collective-permute-start(bf16[8,1,128,1024]{3,2,0,1:T(8,128)(2,1)} %fusion), channel_id=1, source_target_pairs={{0,2},{2,0},{4,6},{6,4},{8,10},{10,8},{12,14},{14,12},{16,18},{18,... | collective-permute-start | bytes 6291464 | tf_op jit(solution)/shard_map/ppermute | solution.py:240
  9.5 25.7 %copy-start.3 = (bf16[256,1152]{1,0:T(8,128)(2,1)}, bf16[256,1152]{1,0:T(8,128)(2,1)S(1)}, u32[]{:S(2)}) copy-start(bf16[256,1152]{1,0:T(8,128)(2,1)S(1)} %pad_maximum_fusion.k_ref.kd_ref.v_ref) | copy-start | bytes 1769476
  9.5 17.7 %collective-permute-start.1 = (bf16[256,1152]{1,0:T(8,128)(2,1)S(1)}, bf16[256,1152]{1,0:T(8,128)(2,1)S(1)}, u32[]{:S(2)}, u32[]{:S(2)}) collective-permute-start(bf16[256,1152]{1,0:T(8,128)(2,1)S(1)} %pad_maximum_fusion.k_ref.kd_ref.v_ref), channel_id=1, source_target_pairs={{0,8},{2,10},{4,12},{6,14},{8,16},{10,18},{12,20},{14,22},{16,24},... | collective-permute-start | bytes 1769480 | tf_op jit(solution)/shard_map/ppermute | solution.py:186
  27.2 8.0 %copy-start.2 = (bf16[256,1152]{1,0:T(8,128)(2,1)}, bf16[256,1152]{1,0:T(8,128)(2,1)S(1)}, u32[]{:S(2)}) copy-start(bf16[256,1152]{1,0:T(8,128)(2,1)S(1)} %collective-permute-done.1.k_ref.kd_ref.v_ref) | copy-start | bytes 1769476
  28.7 80.9 %collective-permute-start.4 = (bf16[256,1152]{1,0:T(8,128)(2,1)}, bf16[256,1152]{1,0:T(8,128)(2,1)S(1)}, u32[]{:S(2)}, u32[]{:S(2)}) collective-permute-start(bf16[256,1152]{1,0:T(8,128)(2,1)} %get-tuple-element.44), channel_id=1, source_target_pairs={{0,2},{2,4},{4,6},{6,0},{8,10},{10,12},{12,14},{14,8},{16,18},{18,... | collective-permute-start | bytes 1769480 | tf_op jit(solution)/shard_map/ppermute | solution.py:179
  28.7 85.7 %collective-permute-start.3 = (bf16[256,1152]{1,0:T(8,128)(2,1)}, bf16[256,1152]{1,0:T(8,128)(2,1)S(1)}, u32[]{:S(2)}, u32[]{:S(2)}) collective-permute-start(bf16[256,1152]{1,0:T(8,128)(2,1)} %get-tuple-element.45), channel_id=1, source_target_pairs={{0,4},{2,6},{4,0},{6,2},{8,12},{10,14},{12,8},{14,10},{16,20},{18,... | collective-permute-start | bytes 1769480 | tf_op jit(solution)/shard_map/ppermute | solution.py:179
  30.2 88.9 %collective-permute-start.2 = (bf16[256,1152]{1,0:T(8,128)(2,1)}, bf16[256,1152]{1,0:T(8,128)(2,1)S(1)}, u32[]{:S(2)}, u32[]{:S(2)}) collective-permute-start(bf16[256,1152]{1,0:T(8,128)(2,1)} %get-tuple-element.46), channel_id=1, source_target_pairs={{0,6},{2,0},{4,2},{6,4},{8,14},{10,8},{12,10},{14,12},{16,22},{18,... | collective-permute-start | bytes 1769480 | tf_op jit(solution)/shard_map/ppermute | solution.py:179
  35.2 2.0 copy-start.1
  35.2 3.6 %copy-start.12 = (s32[16]{0:T(128)S(1)}, s32[16]{0:T(128)}, u32[]{:S(2)}) copy-start(s32[16]{0:T(128)} %param.17) | copy-start | bytes 196
  35.2 3.6 %copy-start.10 = (f32[1,16,128]{2,1,0:T(8,128)S(1)}, f32[1,16,128]{2,1,0:T(8,128)}, u32[]{:S(2)}) copy-start(f32[1,16,128]{2,1,0:T(8,128)} %param.16) | copy-start | bytes 24580
  38.3 108.0 %collective-permute-start.10 = (bf16[4,1,128,1024]{3,2,0,1:T(8,128)(2,1)}, bf16[4,1,128,1024]{3,2,0,1:T(8,128)(2,1)}, u32[]{:S(2)}, u32[]{:S(2)}) collective-permute-start(bf16[4,1,128,1024]{3,2,0,1:T(8,128)(2,1)} %fusion.10), channel_id=1, source_target_pairs={{0,4},{2,6},{4,0},{6,2},{8,12},{10,14},{12,8},{14,10},{16,20},{18,... | collective-permute-start | bytes 3145736 | tf_op jit(solution)/shard_map/ppermute | solution.py:240
  38.9 64.0 %collective-permute-start = (f32[16,128]{1,0:T(8,128)S(1)}, f32[16,128]{1,0:T(8,128)S(1)}, u32[]{:S(2)}, u32[]{:S(2)}) collective-permute-start(f32[16,128]{1,0:T(8,128)S(1)} %bitcast_select_fusion), channel_id=1, source_target_pairs={{0,1},{1,0},{2,3},{3,2},{4,5},{5,4},{6,7},{7,6},{8,9},{9,8},{10,11... | collective-permute-start | bytes 24584 | tf_op jit(solution)/shard_map/ppermute | solution.py:221
  114.4 0.9 copy-start.6
  143.0 12.7 %collective-permute-start.7 = (bf16[2,256,512]{2,1,0:T(8,128)(2,1)}, bf16[2,256,512]{2,1,0:T(8,128)(2,1)S(1)}, u32[]{:S(2)}, u32[]{:S(2)}) collective-permute-start(bf16[2,256,512]{2,1,0:T(8,128)(2,1)} %get-tuple-element.42), channel_id=1, source_target_pairs={{0,2},{2,4},{4,6},{6,0},{8,10},{10,12},{12,14},{14,8},{16,18},{18,... | collective-permute-start | bytes 1572872 | tf_op jit(solution)/shard_map/ppermute | solution.py:179
  143.4 14.0 %collective-permute-start.5 = (bf16[2,256,512]{2,1,0:T(8,128)(2,1)}, bf16[2,256,512]{2,1,0:T(8,128)(2,1)S(1)}, u32[]{:S(2)}, u32[]{:S(2)}) collective-permute-start(bf16[2,256,512]{2,1,0:T(8,128)(2,1)} %get-tuple-element.40), channel_id=1, source_target_pairs={{0,6},{2,0},{4,2},{6,4},{8,14},{10,8},{12,10},{14,12},{16,22},{18,... | collective-permute-start | bytes 1572872 | tf_op jit(solution)/shard_map/ppermute | solution.py:179
  144.8 24.0 %collective-permute-start.6 = (bf16[2,256,512]{2,1,0:T(8,128)(2,1)}, bf16[2,256,512]{2,1,0:T(8,128)(2,1)}, u32[]{:S(2)}, u32[]{:S(2)}) collective-permute-start(bf16[2,256,512]{2,1,0:T(8,128)(2,1)} %get-tuple-element.41), channel_id=1, source_target_pairs={{0,4},{2,6},{4,0},{6,2},{8,12},{10,14},{12,8},{14,10},{16,20},{18,... | collective-permute-start | bytes 1572872 | tf_op jit(solution)/shard_map/ppermute | solution.py:179
  149.4 28.2 %collective-permute-start.11 = (bf16[2,1,128,1024]{3,2,0,1:T(8,128)(2,1)}, bf16[2,1,128,1024]{3,2,0,1:T(8,128)(2,1)}, u32[]{:S(2)}, u32[]{:S(2)}) collective-permute-start(bf16[2,1,128,1024]{3,2,0,1:T(8,128)(2,1)} %fusion.11), channel_id=1, source_target_pairs={{0,8},{2,10},{4,12},{6,14},{8,0},{10,2},{12,4},{14,6},{16,24},{18,... | collective-permute-start | bytes 1572872 | tf_op jit(solution)/shard_map/ppermute | solution.py:240
  171.2 15.2 %collective-permute-start.8 = (bf16[2,256,512]{2,1,0:T(8,128)(2,1)}, bf16[2,256,512]{2,1,0:T(8,128)(2,1)}, u32[]{:S(2)}, u32[]{:S(2)}) collective-permute-start(bf16[2,256,512]{2,1,0:T(8,128)(2,1)} %fusion.9), channel_id=1, source_target_pairs={{8,0},{10,2},{12,4},{14,6},{16,8},{18,10},{20,12},{22,14},{24,16},... | collective-permute-start | bytes 1572872 | tf_op jit(solution)/shard_map/ppermute | solution.py:186
  177.6 8.7 %copy-start.7 = (f32[2,256,512]{2,1,0:T(8,128)S(1)}, f32[2,256,512]{2,1,0:T(8,128)}, u32[]{:S(2)}) copy-start(f32[2,256,512]{2,1,0:T(8,128)} %get-tuple-element.39) | copy-start | bytes 3145732
  178.9 18.6 %collective-permute-start.12 = (bf16[1,1,128,1024]{3,2,0,1:T(8,128)(2,1)S(1)}, bf16[1,1,128,1024]{3,2,0,1:T(8,128)(2,1)S(1)}, u32[]{:S(2)}, u32[]{:S(2)}) collective-permute-start(bf16[1,1,128,1024]{3,2,0,1:T(8,128)(2,1)S(1)} %dynamic-slice_convert_fusion.2), channel_id=1, source_target_pairs={{0,16},{2,18},{4,20},{6,22},{8,24},{10,26},{12,28},{14,30},{16,0},... | collective-permute-start | bytes 786440 | tf_op jit(solution)/shard_map/ppermute | solution.py:240
  (2 other events, 1.6 us)

commit v3 on v2

--- a/solution.py
+++ b/solution.py
@@ -39,15 +39,27 @@
     return jnp.concatenate([allowed.astype(jnp.float32)] * pairs, axis=1) > 0.5
 
 
-def stats_kernel(own, final, pairs, scale, q_ref, k_ref, kd_ref, qd_ref, m_ref, l_ref, *outs):
+def stats_kernel(owns, final, pairs, scale, q_ref, *refs):
+    count = len(owns)
+    blocks = refs[: 2 * count]
+    qd_ref, m_ref, l_ref, *outs = refs[2 * count :]
     rows = q_ref.shape[0]
-    scores = dot(k_ref[...], stacked(q_ref, pairs), LAST) * scale
-    allowed = visible(kd_ref, qd_ref, pairs, own)
-    masked = jnp.where(allowed, scores, LOW)
+    queries = stacked(q_ref, pairs)
+    masked = [
+        jnp.where(
+            visible(blocks[2 * i + 1], qd_ref, pairs, owns[i]),
+            dot(blocks[2 * i][...], queries, LAST) * scale,
+            LOW,
+        )
+        for i in range(count)
+    ]
     highest, running = row_of(m_ref, pairs), row_of(l_ref, pairs)
-    newest = jnp.maximum(highest, jnp.max(masked, axis=0, keepdims=True))
-    weights = jnp.where(allowed, jnp.exp(scores - newest), 0.0)
-    total = running * jnp.exp(highest - newest) + jnp.sum(weights, axis=0, keepdims=True)
+    newest = highest
+    for scores in masked:
+        newest = jnp.maximum(newest, jnp.max(scores, axis=0, keepdims=True))
+    total = running * jnp.exp(highest - newest)
+    for scores in masked:
+        total = total + jnp.sum(jnp.exp(scores - newest), axis=0, keepdims=True)
     results = (newest + jnp.log(total),) if final else (newest, total)
     for out, result in zip(outs, results):
         for j in range(pairs):
@@ -226,10 +238,12 @@
     )
 
     columns = attention_output.shape[1]
-    summed_weight = dot(grad_y, attention_output, FIRST) * (rows * ctx_count) ** (-0.5)
+    summed_weight = (
+        dot(grad_y, attention_output, FIRST) * (rows * ctx_count) ** (-0.5)
+    ).astype(jnp.bfloat16)
     summed_weight = summed_weight.reshape(ctx_count, -1, columns)
     left = list(range(bits))
-    for bit in [0] + list(range(1, bits)):
+    for bit in range(bits):
         shape = summed_weight.shape
         low = 1 << left.index(bit)
         left.remove(bit)
@@ -238,7 +252,7 @@
         kept = lax.dynamic_index_in_dim(split, mine, 1, keepdims=False)
         sent = lax.dynamic_index_in_dim(split, 1 - mine, 1, keepdims=False).astype(jnp.bfloat16)
         got = lax.ppermute(sent, "ctx", [(i, i ^ (1 << bit)) for i in range(ctx_count)])
-        summed_weight = (kept + got.astype(jnp.float32)).reshape(shape[0] // 2, *shape[1:])
+        summed_weight = (kept.astype(jnp.float32) + got.astype(jnp.float32)).reshape(shape[0] // 2, *shape[1:])
     grad_weight = summed_weight[0]
 
     pair_spec = pl.BlockSpec((rows, pairs * HEAD_WIDTH), lambda g: (0, g))
@@ -250,23 +264,29 @@
     row_shape = jax.ShapeDtypeStruct((groups, pairs, rows), jnp.float32)
     tile = 2 * rows * rows * HEAD_WIDTH * heads
 
-    def stats(block, state, own, final):
+    def stats(chunk, state, owns, final):
         count = 1 if final else 2
         return pl.pallas_call(
-            functools.partial(stats_kernel, own, final, pairs, scale),
+            functools.partial(stats_kernel, owns, final, pairs, scale),
             grid=(groups,),
-            in_specs=[pair_spec, key_spec, docs_spec, query_docs_spec, row_spec, row_spec],
+            in_specs=[pair_spec]
+            + [key_spec, docs_spec] * len(chunk)
+            + [query_docs_spec, row_spec, row_spec],
             out_specs=[row_spec] * count,
             out_shape=[row_shape] * count,
             cost_estimate=pl.CostEstimate(
-                flops=2 * tile, bytes_accessed=1 << 20, transcendentals=rows * rows * heads
+                flops=2 * tile * len(chunk),
+                bytes_accessed=len(chunk) << 20,
+                transcendentals=rows * rows * heads * len(chunk),
             ),
             name="stats",
-        )(query, block, block, query_docs, *state)
+        )(query, *[block for block in chunk for _ in range(2)], query_docs, *state)
 
     state = [jnp.full(row_shape.shape, LOW, jnp.float32), jnp.zeros(row_shape.shape, jnp.float32)]
-    for d in range(steps):
-        state = stats(blocks[d], state, d == 0, d == steps - 1)
+    state = stats(blocks[:1], state, (True,), False)
+    for start in range(1, steps, 4):
+        chunk = blocks[start : start + 4]
+        state = stats(chunk, state, (False,) * len(chunk), start + 4 >= steps)
     log_total = state[0]
 
     if codes.shape[1] % HEAD_WIDTH == 0:

time: 199 us -> 185 us (0.930)
  Pallas kernels: 108 us -> 99.4 us
  local copies, waits for them, and re-layouts: 14.6 us -> 9.93 us
    pallas_call x5 -> x2, Pallas kernels: 19.4 us -> 9.38 us  [stats(): pl.pallas_call(functools.partial(stats_kernel, owns, final, pairs, scale)...]
    unnamed x26, local copies, waits for them, and re-layouts: 7.72 us -> 4.11 us
    convert_element_type x4 -> x3, local copies, waits for them, and re-layouts: 3.76 us -> 1.08 us  [per_device(): lax.dynamic_index_in_dim(split, 1 - mine, 1, keepdims=False)]
where the time goes in v3:
time: 185 us
  Pallas kernels  99.4 us (54%)
  waiting for transfers between devices  40.2 us (22%)
  starting transfers between devices  18 us (10%)
  other arithmetic  13.5 us (7%)
  local copies, waits for them, and re-layouts  9.93 us (5%)
  matrix products  2.65 us (1%)
    pallas_call x1, Pallas kernels, gather(): pl.pallas_call(functools.partial(gather_kernel, count), out_shape=jax.Sha...  58.8 us
    pallas_call x5, Pallas kernels, grads(): pl.pallas_call(functools.partial(grads_kernel, own, first, pairs, scale),...  25.6 us
    ppermute x2, waiting for transfers between devices, shift_by(): lax.ppermute(x, axis, [(i, i + by) for i in range(size) if 0 <= i + by <...  17.1 us
    ppermute x6, waiting for transfers between devices, plane_turn(): lax.ppermute(x, 'ctx', [(i, i // plane * plane + (i % plane + by) % plane...  14.2 us
    pallas_call x2, Pallas kernels, stats(): pl.pallas_call(functools.partial(stats_kernel, owns, final, pairs, scale)...  9.38 us
    ppermute x4, waiting for transfers between devices, per_device(): lax.ppermute(sent, 'ctx', [(i, i ^ 1 << bit) for i in range(ctx_count)])  8.84 us
    add x3, other arithmetic, per_device(): kept.astype(jnp.float32) + got.astype(jnp.float32)  6.62 us
    ppermute x6, starting transfers between devices, plane_turn(): lax.ppermute(x, 'ctx', [(i, i // plane * plane + (i % plane + by) % plane...  6.31 us
  transfers between devices with their start and end apart: 13, of which 6 were waited for; matrix products, arithmetic and copies ran while one was open for 9% of the time, Pallas kernels for 54%

profile of v3, /device:TPU:0, one launch (start us, length us, event | category | flops | bytes accessed | tf_op | source)
XLA Modules:
  0.0 184.6 jit_solution(14859885042562812712)
XLA Ops:
  0.6 2.6 %multiply_convert_fusion = bf16[2048,1024]{1,0:T(8,128)(2,1)S(1)} fusion(bf16[256,2048]{1,0:T(8,128)(2,1)} %y_ref.1, bf16[256,1024]{1,0:T(8,128)(2,1)} %o_ref.1), kind=kOutput, calls=%fused_computation | convolution fusion | flops 1077936128 | bytes 5767168 | tf_op jit(solution)/shard_map/dot_general | solution.py:17
  3.3 1.6 dynamic-slice_bitcast_fusion
  7.2 4.5 %collective-permute-start.1 = (bf16[256,1152]{1,0:T(8,128)(2,1)S(1)}, bf16[256,1152]{1,0:T(8,128)(2,1)S(1)}, u32[]{:S(2)}, u32[]{:S(2)}) collective-permute-start(bf16[256,1152]{1,0:T(8,128)(2,1)S(1)} %pad_maximum_fusion.refs_0_.refs_1_.k_ref.v_ref.kd_ref), channel_id=1, source_target_pairs={{0,8},{2,10},{4,12},{6,14},{8,16},{10,18},{12,20},{14,22},{16,24},... | collective-permute-start | bytes 1769480 | tf_op jit(solution)/shard_map/ppermute | solution.py:198
  11.7 13.1 %collective-permute-done.1.refs_6_.refs_7_.k_ref.v_ref.kd_ref = bf16[256,1152]{1,0:T(8,128)(2,1)S(1)} collective-permute-done((bf16[256,1152]{1,0:T(8,128)(2,1)S(1)}, bf16[256,1152]{1,0:T(8,128)(2,1)S(1)}, u32[]{:S(2)}, u32[]{:S(2)}) %collective-permute-start.1) | collective-permute-done | bytes 589856 | tf_op jit(solution)/shard_map/ppermute | solution.py:198
  29.2 3.1 %convert_add_fusion = f32[8,1,128,1024]{3,2,0,1:T(8,128)S(1)} fusion(bf16[8,1,128,1024]{3,2,0,1:T(8,128)(2,1)} %collective-permute-done.9, bf16[8,2,1,128,1024]{4,3,1,0,2:T(8,128)(2,1)} %bitcast.35, s32[]{:T(128)S(6)} %select_n.149), kind=kLoop, calls=%fused_computation.1 | loop fusion | flops 3145728 | bytes 8388612 | tf_op jit(solution)/shard_map/add | solution.py:255
  32.4 1.9 %copy-done = f32[8,1,128,1024]{3,2,0,1:T(8,128)} copy-done((f32[8,1,128,1024]{3,2,0,1:T(8,128)}, f32[8,1,128,1024]{3,2,0,1:T(8,128)S(1)}, u32[]{:S(2)}) %copy-start) | copy-done | bytes 4194328
  37.8 3.8 %stats.2 = (f32[4,2,256]{2,1,0:T(2,128)}, f32[4,2,256]{2,1,0:T(2,128)}) custom-call(bf16[256,1024]{1,0:T(8,128)(2,1)} %q_ref.13, bf16[256,1152]{1,0:T(8,128)(2,1)} %copy-done.1, bf16[256,1152]{1,0:T(8,128)(2,1)} %copy-done.1, f32[1,256]{1,0:T(1,128)} %bitcast.37, f32[4,2,256]{2,1,0:T(2,128)} %broadcast_in_dim.41.refs_3_, f32[4,2,256]{2,1,0:T(2,128)} %broadcast_in_dim.42.refs_4_), custom_call_target="tpu_custom_call" | custom-call | flops 268435456 | bytes 1048576 | tf_op jit(solution)/shard_map/stats/pallas_call | solution.py:269
  41.6 58.8 %gather.1.code_ref = bf16[16,1024,128]{2,1,0:T(8,128)(2,1)} custom-call(bf16[1024,128]{1,0:T(8,128)(2,1)} %code_ref.1), custom_call_target="tpu_custom_call" | custom-call | bytes 104857600 | tf_op jit(solution)/shard_map/gather/pallas_call | solution.py:160
  101.5 5.6 %project.1 = (bf16[256,1024]{1,0:T(8,128)(2,1)}, f32[4,2,256]{2,1,0:T(2,128)}) custom-call(bf16[256,2048]{1,0:T(8,128)(2,1)} %y_ref.1, bf16[16,1024,128]{2,1,0:T(8,128)(2,1)} %gather.1.code_ref, f32[1024,1]{1,0:T(8,128)} %copy.14.scale_ref, bf16[256,1024]{1,0:T(8,128)(2,1)} %o_ref.1), custom_call_target="tpu_custom_call" | custom-call | flops 1073741824 | bytes 6291456 | tf_op jit(solution)/shard_map/project/pallas_call | solution.py:293
  108.3 5.6 %stats.3.t_ref = f32[4,2,256]{2,1,0:T(2,128)} custom-call(bf16[256,1024]{1,0:T(8,128)(2,1)} %q_ref.13, bf16[256,1152]{1,0:T(8,128)(2,1)} %copy-done.4, bf16[256,1152]{1,0:T(8,128)(2,1)} %copy-done.4, bf16[256,1152]{1,0:T(8,128)(2,1)} %copy-done.6, bf16[256,1152]{1,0:T(8,128)(2,1)} %copy-done.6, bf16[256,1152]{1,0:T(8,128)(2,1)} %copy-done.5, ...), custom_call_target="tpu_custom_call" | custom-call | flops 1073741824 | bytes 4194304 | tf_op jit(solution)/shard_map/stats/pallas_call | solution.py:269
  113.9 4.9 %grads.5 = (f32[256,1024]{1,0:T(8,128)}, bf16[2,256,512]{2,1,0:T(8,128)(2,1)}) custom-call(bf16[256,1024]{1,0:T(8,128)(2,1)} %q_ref.13, bf16[256,1024]{1,0:T(8,128)(2,1)} %get-tuple-element.18.a_ref, bf16[256,1152]{1,0:T(8,128)(2,1)} %copy-done.6, bf16[256,1152]{1,0:T(8,128)(2,1)} %copy-done.6, bf16[256,1152]{1,0:T(8,128)(2,1)} %copy-done.6, ...), custom_call_target="tpu_custom_call" | custom-call | flops 1342177280 | bytes 4194304 | tf_op jit(solution)/shard_map/grads/pallas_call | solution.py:327
  118.8 5.2 %grads.6 = (f32[256,1024]{1,0:T(8,128)}, bf16[2,256,512]{2,1,0:T(8,128)(2,1)}) custom-call(bf16[256,1024]{1,0:T(8,128)(2,1)} %q_ref.13, bf16[256,1024]{1,0:T(8,128)(2,1)} %get-tuple-element.18.a_ref, bf16[256,1152]{1,0:T(8,128)(2,1)} %copy-done.4, bf16[256,1152]{1,0:T(8,128)(2,1)} %copy-done.4, bf16[256,1152]{1,0:T(8,128)(2,1)} %copy-done.4, ...), custom_call_target="tpu_custom_call" | custom-call | flops 1342177280 | bytes 4194304 | tf_op jit(solution)/shard_map/grads/pallas_call | solution.py:327
  124.0 5.2 %grads.7 = (f32[256,1024]{1,0:T(8,128)}, bf16[2,256,512]{2,1,0:T(8,128)(2,1)}) custom-call(bf16[256,1024]{1,0:T(8,128)(2,1)} %q_ref.13, bf16[256,1024]{1,0:T(8,128)(2,1)} %get-tuple-element.18.a_ref, bf16[256,1152]{1,0:T(8,128)(2,1)} %copy-done.5, bf16[256,1152]{1,0:T(8,128)(2,1)} %copy-done.5, bf16[256,1152]{1,0:T(8,128)(2,1)} %copy-done.5, ...), custom_call_target="tpu_custom_call" | custom-call | flops 1342177280 | bytes 4194304 | tf_op jit(solution)/shard_map/grads/pallas_call | solution.py:327
  131.0 1.5 collective-permute-start.6
  132.5 2.2 %bitcast_add_fusion = f32[4,1,128,1024]{3,2,0,1:T(8,128)S(1)} fusion(bf16[4,1,128,1024]{3,2,0,1:T(8,128)(2,1)} %collective-permute-done.10, f32[4,2,1,128,1024]{4,3,1,0,2:T(8,128)} %bitcast.31, s32[]{:T(128)S(6)} %select_n.153), kind=kLoop, calls=%fused_computation.2 | loop fusion | flops 1048576 | bytes 5242884 | tf_op jit(solution)/shard_map/add | solution.py:255
  135.6 5.2 %grads.8 = (f32[256,1024]{1,0:T(8,128)}, bf16[2,256,512]{2,1,0:T(8,128)(2,1)}) custom-call(bf16[256,1024]{1,0:T(8,128)(2,1)} %q_ref.13, bf16[256,1024]{1,0:T(8,128)(2,1)} %get-tuple-element.18.a_ref, bf16[256,1152]{1,0:T(8,128)(2,1)} %copy-done.2, bf16[256,1152]{1,0:T(8,128)(2,1)} %copy-done.2, bf16[256,1152]{1,0:T(8,128)(2,1)} %copy-done.2, ...), custom_call_target="tpu_custom_call" | custom-call | flops 1342177280 | bytes 4194304 | tf_op jit(solution)/shard_map/grads/pallas_call | solution.py:327
  141.8 1.8 collective-permute-done.5
  143.6 11.4 %collective-permute-done.6 = bf16[2,256,512]{2,1,0:T(8,128)(2,1)} collective-permute-done((bf16[2,256,512]{2,1,0:T(8,128)(2,1)}, bf16[2,256,512]{2,1,0:T(8,128)(2,1)}, u32[]{:S(2)}, u32[]{:S(2)}) %collective-permute-start.6) | collective-permute-done | bytes 524320 | tf_op jit(solution)/shard_map/ppermute | solution.py:191
  155.0 2.4 %fusion.8 = bf16[2,256,512]{2,1,0:T(8,128)(2,1)} fusion(bf16[2,256,512]{2,1,0:T(8,128)(2,1)S(1)} %collective-permute-done.5, bf16[2,256,512]{2,1,0:T(8,128)(2,1)} %collective-permute-done.6, bf16[2,256,512]{2,1,0:T(8,128)(2,1)S(1)} %collective-permute-done.7, bf16[2,256,512]{2,1,0:T(8,128)(2,1)} %get-tuple-element.31, pred[]{:T(512)S(6)} %ge.11, ...), kind=kLoop, calls=%fused_computation.19 | loop fusion | flops 2883584 | bytes 2621443 | tf_op jit(solution)/shard_map/convert_element_type | solution.py:365
  158.7 5.2 %grads.9 = (bf16[256,1024]{1,0:T(8,128)(2,1)}, f32[2,256,512]{2,1,0:T(8,128)}) custom-call(bf16[256,1024]{1,0:T(8,128)(2,1)} %q_ref.13, bf16[256,1024]{1,0:T(8,128)(2,1)} %get-tuple-element.18.a_ref, bf16[256,1152]{1,0:T(8,128)(2,1)} %copy-done.1, bf16[256,1152]{1,0:T(8,128)(2,1)} %copy-done.1, bf16[256,1152]{1,0:T(8,128)(2,1)} %copy-done.1, ...), custom_call_target="tpu_custom_call" | custom-call | flops 1342177280 | bytes 4194304 | tf_op jit(solution)/shard_map/grads/pallas_call | solution.py:327
  165.2 3.3 %collective-permute-start.12 = (bf16[1,1,128,1024]{3,2,0,1:T(8,128)(2,1)S(1)}, bf16[1,1,128,1024]{3,2,0,1:T(8,128)(2,1)S(1)}, u32[]{:S(2)}, u32[]{:S(2)}) collective-permute-start(bf16[1,1,128,1024]{3,2,0,1:T(8,128)(2,1)S(1)} %dynamic-slice_convert_fusion.2), channel_id=1, source_target_pairs={{0,16},{2,18},{4,20},{6,22},{8,24},{10,26},{12,28},{14,30},{16,0},... | collective-permute-start | bytes 786440 | tf_op jit(solution)/shard_map/ppermute | solution.py:254
  168.5 4.0 %collective-permute-done.8 = bf16[2,256,512]{2,1,0:T(8,128)(2,1)} collective-permute-done((bf16[2,256,512]{2,1,0:T(8,128)(2,1)}, bf16[2,256,512]{2,1,0:T(8,128)(2,1)}, u32[]{:S(2)}, u32[]{:S(2)}) %collective-permute-start.8) | collective-permute-done | bytes 524320 | tf_op jit(solution)/shard_map/ppermute | solution.py:198
  172.5 1.7 fusion.4
  175.0 8.8 %collective-permute-done.12 = bf16[1,1,128,1024]{3,2,0,1:T(8,128)(2,1)S(1)} collective-permute-done((bf16[1,1,128,1024]{3,2,0,1:T(8,128)(2,1)S(1)}, bf16[1,1,128,1024]{3,2,0,1:T(8,128)(2,1)S(1)}, u32[]{:S(2)}, u32[]{:S(2)}) %collective-permute-start.12) | collective-permute-done | bytes 262176 | tf_op jit(solution)/shard_map/ppermute | solution.py:254
  (59 shorter events, 20.2 us)
Async XLA Ops:
  3.3 2.6 %copy-start.3 = (bf16[2048,1024]{1,0:T(8,128)(2,1)}, bf16[2048,1024]{1,0:T(8,128)(2,1)S(1)}, u32[]{:S(2)}) copy-start(bf16[2048,1024]{1,0:T(8,128)(2,1)S(1)} %multiply_convert_fusion) | copy-start | bytes 12582916
  3.3 3.1 %copy-start.11 = (s32[256]{0:T(256)S(1)}, s32[256]{0:T(256)}, u32[]{:S(2)}) copy-start(s32[256]{0:T(256)} %param.14) | copy-start | bytes 3076
  3.3 3.8 %copy-start.8 = (bf16[256,512]{1,0:T(8,128)(2,1)S(1)}, bf16[256,512]{1,0:T(8,128)(2,1)}, u32[]{:S(2)}) copy-start(bf16[256,512]{1,0:T(8,128)(2,1)} %param.11) | copy-start | bytes 786436
  3.3 3.8 %copy-start.9 = (bf16[256,512]{1,0:T(8,128)(2,1)S(1)}, bf16[256,512]{1,0:T(8,128)(2,1)}, u32[]{:S(2)}) copy-start(bf16[256,512]{1,0:T(8,128)(2,1)} %param.10) | copy-start | bytes 786436
  5.9 23.3 %collective-permute-start.9 = (bf16[8,1,128,1024]{3,2,0,1:T(8,128)(2,1)}, bf16[8,1,128,1024]{3,2,0,1:T(8,128)(2,1)}, u32[]{:S(2)}, u32[]{:S(2)}) collective-permute-start(bf16[8,1,128,1024]{3,2,0,1:T(8,128)(2,1)} %dynamic-slice_bitcast_fusion), channel_id=1, source_target_pairs={{0,2},{2,0},{4,6},{6,4},{8,10},{10,8},{12,14},{14,12},{16,18},{18,... | collective-permute-start | bytes 6291464 | tf_op jit(solution)/shard_map/ppermute | solution.py:254
  7.2 25.2 %copy-start.1 = (bf16[256,1152]{1,0:T(8,128)(2,1)}, bf16[256,1152]{1,0:T(8,128)(2,1)S(1)}, u32[]{:S(2)}) copy-start(bf16[256,1152]{1,0:T(8,128)(2,1)S(1)} %pad_maximum_fusion.refs_0_.refs_1_.k_ref.v_ref.kd_ref) | copy-start | bytes 1769476
  7.2 17.7 %collective-permute-start.1 = (bf16[256,1152]{1,0:T(8,128)(2,1)S(1)}, bf16[256,1152]{1,0:T(8,128)(2,1)S(1)}, u32[]{:S(2)}, u32[]{:S(2)}) collective-permute-start(bf16[256,1152]{1,0:T(8,128)(2,1)S(1)} %pad_maximum_fusion.refs_0_.refs_1_.k_ref.v_ref.kd_ref), channel_id=1, source_target_pairs={{0,8},{2,10},{4,12},{6,14},{8,16},{10,18},{12,20},{14,22},{16,24},... | collective-permute-start | bytes 1769480 | tf_op jit(solution)/shard_map/ppermute | solution.py:198
  24.9 7.4 %copy-start.2 = (bf16[256,1152]{1,0:T(8,128)(2,1)}, bf16[256,1152]{1,0:T(8,128)(2,1)S(1)}, u32[]{:S(2)}) copy-start(bf16[256,1152]{1,0:T(8,128)(2,1)S(1)} %collective-permute-done.1.refs_6_.refs_7_.k_ref.v_ref.kd_ref) | copy-start | bytes 1769476
  26.2 80.9 %collective-permute-start.2 = (bf16[256,1152]{1,0:T(8,128)(2,1)}, bf16[256,1152]{1,0:T(8,128)(2,1)S(1)}, u32[]{:S(2)}, u32[]{:S(2)}) collective-permute-start(bf16[256,1152]{1,0:T(8,128)(2,1)} %get-tuple-element.34), channel_id=1, source_target_pairs={{0,2},{2,4},{4,6},{6,0},{8,10},{10,12},{12,14},{14,8},{16,18},{18,... | collective-permute-start | bytes 1769480 | tf_op jit(solution)/shard_map/ppermute | solution.py:191
  26.2 80.9 %collective-permute-start.3 = (bf16[256,1152]{1,0:T(8,128)(2,1)}, bf16[256,1152]{1,0:T(8,128)(2,1)S(1)}, u32[]{:S(2)}, u32[]{:S(2)}) collective-permute-start(bf16[256,1152]{1,0:T(8,128)(2,1)} %get-tuple-element.33), channel_id=1, source_target_pairs={{0,4},{2,6},{4,0},{6,2},{8,12},{10,14},{12,8},{14,10},{16,20},{18,... | collective-permute-start | bytes 1769480 | tf_op jit(solution)/shard_map/ppermute | solution.py:191
  27.7 79.4 %collective-permute-start.4 = (bf16[256,1152]{1,0:T(8,128)(2,1)S(1)}, bf16[256,1152]{1,0:T(8,128)(2,1)S(1)}, u32[]{:S(2)}, u32[]{:S(2)}) collective-permute-start(bf16[256,1152]{1,0:T(8,128)(2,1)S(1)} %get-tuple-element.32), channel_id=1, source_target_pairs={{0,6},{2,0},{4,2},{6,4},{8,14},{10,8},{12,10},{14,12},{16,22},{18,... | collective-permute-start | bytes 1769480 | tf_op jit(solution)/shard_map/ppermute | solution.py:191
  32.3 2.0 %copy-start = (f32[8,1,128,1024]{3,2,0,1:T(8,128)}, f32[8,1,128,1024]{3,2,0,1:T(8,128)S(1)}, u32[]{:S(2)}) copy-start(f32[8,1,128,1024]{3,2,0,1:T(8,128)S(1)} %convert_add_fusion) | copy-start | bytes 12582916
  32.3 2.7 %copy-start.12 = (s32[16]{0:T(128)S(1)}, s32[16]{0:T(128)}, u32[]{:S(2)}) copy-start(s32[16]{0:T(128)} %param.17) | copy-start | bytes 196
  32.4 2.7 %copy-start.10 = (f32[1,16,128]{2,1,0:T(8,128)S(1)}, f32[1,16,128]{2,1,0:T(8,128)}, u32[]{:S(2)}) copy-start(f32[1,16,128]{2,1,0:T(8,128)} %param.16) | copy-start | bytes 24580
  34.5 98.0 %collective-permute-start.10 = (bf16[4,1,128,1024]{3,2,0,1:T(8,128)(2,1)S(1)}, bf16[4,1,128,1024]{3,2,0,1:T(8,128)(2,1)}, u32[]{:S(2)}, u32[]{:S(2)}) collective-permute-start(bf16[4,1,128,1024]{3,2,0,1:T(8,128)(2,1)S(1)} %fusion.9), channel_id=1, source_target_pairs={{0,4},{2,6},{4,0},{6,2},{8,12},{10,14},{12,8},{14,10},{16,20},{18,... | collective-permute-start | bytes 3145736 | tf_op jit(solution)/shard_map/ppermute | solution.py:254
  35.1 65.3 %collective-permute-start = (f32[16,128]{1,0:T(8,128)S(1)}, f32[16,128]{1,0:T(8,128)S(1)}, u32[]{:S(2)}, u32[]{:S(2)}) collective-permute-start(f32[16,128]{1,0:T(8,128)S(1)} %bitcast_select_fusion), channel_id=1, source_target_pairs={{0,1},{1,0},{2,3},{3,2},{4,5},{5,4},{6,7},{7,6},{8,9},{9,8},{10,11... | collective-permute-start | bytes 24584 | tf_op jit(solution)/shard_map/ppermute | solution.py:233
  107.2 1.2 copy-start.5
  129.2 12.7 %collective-permute-start.7 = (bf16[2,256,512]{2,1,0:T(8,128)(2,1)}, bf16[2,256,512]{2,1,0:T(8,128)(2,1)S(1)}, u32[]{:S(2)}, u32[]{:S(2)}) collective-permute-start(bf16[2,256,512]{2,1,0:T(8,128)(2,1)} %get-tuple-element.30), channel_id=1, source_target_pairs={{0,2},{2,4},{4,6},{6,0},{8,10},{10,12},{12,14},{14,8},{16,18},{18,... | collective-permute-start | bytes 1572872 | tf_op jit(solution)/shard_map/ppermute | solution.py:191
  129.6 14.0 %collective-permute-start.5 = (bf16[2,256,512]{2,1,0:T(8,128)(2,1)}, bf16[2,256,512]{2,1,0:T(8,128)(2,1)S(1)}, u32[]{:S(2)}, u32[]{:S(2)}) collective-permute-start(bf16[2,256,512]{2,1,0:T(8,128)(2,1)} %get-tuple-element.28), channel_id=1, source_target_pairs={{0,6},{2,0},{4,2},{6,4},{8,14},{10,8},{12,10},{14,12},{16,22},{18,... | collective-permute-start | bytes 1572872 | tf_op jit(solution)/shard_map/ppermute | solution.py:191
  131.0 24.0 %collective-permute-start.6 = (bf16[2,256,512]{2,1,0:T(8,128)(2,1)}, bf16[2,256,512]{2,1,0:T(8,128)(2,1)}, u32[]{:S(2)}, u32[]{:S(2)}) collective-permute-start(bf16[2,256,512]{2,1,0:T(8,128)(2,1)} %get-tuple-element.29), channel_id=1, source_target_pairs={{0,4},{2,6},{4,0},{6,2},{8,12},{10,14},{12,8},{14,10},{16,20},{18,... | collective-permute-start | bytes 1572872 | tf_op jit(solution)/shard_map/ppermute | solution.py:191
  135.6 28.3 %collective-permute-start.11 = (bf16[2,1,128,1024]{3,2,0,1:T(8,128)(2,1)}, bf16[2,1,128,1024]{3,2,0,1:T(8,128)(2,1)}, u32[]{:S(2)}, u32[]{:S(2)}) collective-permute-start(bf16[2,1,128,1024]{3,2,0,1:T(8,128)(2,1)} %fusion.10), channel_id=1, source_target_pairs={{0,8},{2,10},{4,12},{6,14},{8,0},{10,2},{12,4},{14,6},{16,24},{18,... | collective-permute-start | bytes 1572872 | tf_op jit(solution)/shard_map/ppermute | solution.py:254
  157.3 15.1 %collective-permute-start.8 = (bf16[2,256,512]{2,1,0:T(8,128)(2,1)}, bf16[2,256,512]{2,1,0:T(8,128)(2,1)}, u32[]{:S(2)}, u32[]{:S(2)}) collective-permute-start(bf16[2,256,512]{2,1,0:T(8,128)(2,1)} %fusion.8), channel_id=1, source_target_pairs={{8,0},{10,2},{12,4},{14,6},{16,8},{18,10},{20,12},{22,14},{24,16},... | collective-permute-start | bytes 1572872 | tf_op jit(solution)/shard_map/ppermute | solution.py:198
  163.8 8.7 %copy-start.7 = (f32[2,256,512]{2,1,0:T(8,128)S(1)}, f32[2,256,512]{2,1,0:T(8,128)}, u32[]{:S(2)}) copy-start(f32[2,256,512]{2,1,0:T(8,128)} %get-tuple-element.27) | copy-start | bytes 3145732
  165.2 18.6 %collective-permute-start.12 = (bf16[1,1,128,1024]{3,2,0,1:T(8,128)(2,1)S(1)}, bf16[1,1,128,1024]{3,2,0,1:T(8,128)(2,1)S(1)}, u32[]{:S(2)}, u32[]{:S(2)}) collective-permute-start(bf16[1,1,128,1024]{3,2,0,1:T(8,128)(2,1)S(1)} %dynamic-slice_convert_fusion.2), channel_id=1, source_target_pairs={{0,16},{2,18},{4,20},{6,22},{8,24},{10,26},{12,28},{14,30},{16,0},... | collective-permute-start | bytes 786440 | tf_op jit(solution)/shard_map/ppermute | solution.py:254
  (2 other events, 1.9 us)
